TPU v7x, 32 devices: a whole 2x2x4 slice. The times are simulated.
32 devices in a mesh: blk: 4 (over y, x), ulys: 8 (over z, core).
Axes of the slice: x: 2, y: 2, z: 4, core: 2. Of those that a mesh axis runs over, the one named last changes fastest.
Arguments:
- mamba_input: bfloat16 [8192, 16384], P(('blk', 'ulys')), may hold values from -6 to 6
- gate_input: bfloat16 [8192, 16384], P(('blk', 'ulys')), may hold values from -6 to 6
- delta_low: bfloat16 [8192, 512], P(('blk', 'ulys')), may hold values from -12 to 12
- state_mixers: bfloat16 [8192, 32], P(('blk', 'ulys')), may hold values from -6 to 6
- conv_weight: bfloat16 [4, 16384], P(None, 'ulys'), may hold values from -3 to 3
- conv_bias: float32 [16384], P('ulys'), may hold values from -3 to 3
- delta_weight: bfloat16 [512, 16384], P(None, 'ulys'), may hold values from -0.25 to 0.25
- delta_bias: float32 [16384], P('ulys'), may hold values from -12 to -2.3
- decay_log: float32 [16, 16384], P(None, 'ulys'), may hold values from -1 to 2.7
- skip_gain: float32 [16384], P('ulys'), may hold values from 0.5 to 1.5
- queries: bfloat16 [8192, 4096], P(('blk', 'ulys')), may hold values from -4.5 to 4.5
- key_rows: bfloat16 [8192, 1024], P(('blk', 'ulys')), may hold values from -4.5 to 4.5
- value_rows: bfloat16 [8192, 1024], P(('blk', 'ulys')), may hold values from -6 to 6
- span_order: int32 [8], replicated, may hold values from 0 to 7, as said below
Outputs:
- mamba_output: bfloat16 [8192, 16384], P(('blk', 'ulys'))
- attention_output: bfloat16 [8192, 4096], P(('blk', 'ulys'))
Inputs may be any that keep to these rules, and one draw needn't show every extreme that they name: `span_order`: device i of blk holds stored blocks 2i and 2i+1, whose sequence places are p and 7 - p for some p below 4, in either order; every sequence place appears once; the device holding places 0 and 7 and the device holding places 1 and 6 are 2 apart along blk.
All inputs are finite; a program needn't handle non-finite values.
Results may differ from a plain program's by a relative error of at most 0.013.
Values may be sent and summed in bfloat16 or wider, within the bound.
No kernel may reach another device: no remote copies, remote signals or barrier semaphores. Data moves between devices by JAX's collectives and lax.ppermute only.
A program may use at most 192 MiB of HBM per device.

v0:
```python
import jax
import jax.numpy as jnp
from jax import lax
from jax.sharding import PartitionSpec as P

STATE = 16
CONV = 4
HD = 128
SPAN = 1024


NEG_LARGE = -1e30


def token_major(array_in):
    return jnp.swapaxes(array_in, 0, 1)


def row_offsets(row_index, span_order):
    stored_block = row_index // SPAN
    places = jnp.arange(span_order.shape[0], dtype=jnp.int32)
    matches = stored_block[:, None] == places[None, :]
    first_pos = jnp.sum(jnp.where(matches, span_order[None, :], 0), axis=1)
    return first_pos * SPAN + row_index % SPAN


def token_scan(start_state, steps_in, decay_rates):

    def advance(hidden, inputs):
        delta_now, driven_now, inject_now, readout_now = inputs
        hidden = (
            jnp.exp(delta_now[:, None, :] * decay_rates[None]) * hidden
            + (delta_now * driven_now)[:, None, :] * inject_now[:, :, None]
        )
        return (hidden, jnp.sum(readout_now[:, :, None] * hidden, axis=1))

    return lax.scan(advance, start_state, steps_in, unroll=8)


def absorb(carried, query_part, query_pos, key_block, value_block, key_pos, score_scale):
    running_max, running_sum, running_acc = carried
    scores = (
        jnp.einsum("qhd,kd->hqk", query_part, key_block, preferred_element_type=jnp.float32)
        * score_scale
    )
    allowed = key_pos[None, None, :] <= query_pos[None, :, None]
    new_max = jnp.maximum(running_max, jnp.max(jnp.where(allowed, scores, NEG_LARGE), axis=2))
    weights = jnp.where(allowed, jnp.exp(scores - new_max[:, :, None]), 0.0)
    shrink = jnp.exp(running_max - new_max)
    new_sum = running_sum * shrink + jnp.sum(weights, axis=2)
    new_acc = running_acc * shrink[:, :, None] + jnp.einsum(
        "hqk,kd->hqd", weights.astype(jnp.bfloat16), value_block, preferred_element_type=jnp.float32
    )
    return (new_max, new_sum, new_acc)


def local(
    mamba_input,
    gate_input,
    delta_low,
    state_mixers,
    conv_weight,
    conv_bias,
    delta_weight,
    delta_bias,
    decay_log,
    skip_gain,
    queries,
    key_rows,
    value_rows,
    span_order,
):
    cycle_place = lax.axis_index("blk")
    block_total = span_order.shape[0]
    input_local = lax.all_to_all(mamba_input, "ulys", split_axis=1, concat_axis=0, tiled=True)
    low_local, mixers_local = (
        lax.all_gather(delta_low, "ulys", axis=0, tiled=True),
        lax.all_gather(state_mixers, "ulys", axis=0, tiled=True),
    )
    col_count = input_local.shape[1]
    input_blocks = input_local.reshape(2, SPAN, col_count)
    my_blocks = lax.dynamic_slice_in_dim(span_order, 2 * cycle_place, 2, 0)
    tail_rows = lax.all_gather(input_blocks[:, SPAN - (CONV - 1) :, :], "blk", axis=0, tiled=True)
    follows = (span_order[None, :] == my_blocks[:, None] - 1).astype(jnp.bfloat16)
    prior_state = jnp.einsum("cj,jtk->ctk", follows, tail_rows, preferred_element_type=jnp.float32)
    padded = jnp.concatenate([prior_state, input_blocks.astype(jnp.float32)], axis=1)
    mixed_sum = jnp.broadcast_to(conv_bias[None, None, :], (2, SPAN, col_count))
    for offset in range(CONV):
        mixed_sum = (
            mixed_sum
            + conv_weight[offset].astype(jnp.float32)[None, None, :]
            * padded[:, offset : offset + SPAN]
        )
    driven = jax.nn.silu(mixed_sum)
    delta_step = jax.nn.softplus(
        jnp.dot(low_local, delta_weight, preferred_element_type=jnp.float32) + delta_bias[None, :]
    ).reshape(2, SPAN, col_count)
    mixers_blocks = mixers_local.astype(jnp.float32).reshape(2, SPAN, 2 * STATE)
    decay_rates = -jnp.exp(decay_log)
    steps_in = (
        token_major(delta_step),
        token_major(driven),
        token_major(mixers_blocks[:, :, :STATE]),
        token_major(mixers_blocks[:, :, STATE:]),
    )
    local_end, scanned = token_scan(
        jnp.zeros((2, STATE, col_count), jnp.float32), steps_in, decay_rates
    )
    whole_decay = jnp.exp(jnp.sum(delta_step, axis=1)[:, None, :] * decay_rates[None])
    all_decay, all_end = (
        lax.all_gather(whole_decay.astype(jnp.bfloat16), "blk", axis=0, tiled=True).astype(
            whole_decay.dtype
        ),
        lax.all_gather(local_end.astype(jnp.bfloat16), "blk", axis=0, tiled=True).astype(
            local_end.dtype
        ),
    )
    places = jnp.arange(block_total, dtype=jnp.int32)
    holder = jnp.sum(jnp.where(span_order[None, :] == places[:, None], places[None, :], 0), axis=1)

    def carry_on(hidden, position):
        stored_index = lax.dynamic_index_in_dim(holder, position, 0, False)
        decay_here = lax.dynamic_index_in_dim(all_decay, stored_index, 0, False)
        end_here = lax.dynamic_index_in_dim(all_end, stored_index, 0, False)
        return (decay_here * hidden + end_here, hidden)

    _, entering = lax.scan(carry_on, jnp.zeros((STATE, col_count), jnp.float32), places)
    gathered_values = my_blocks[:, None] == places[None, :]
    start_state = jnp.sum(jnp.where(gathered_values[:, :, None, None], entering[None], 0.0), axis=1)
    running_delta = jnp.cumsum(delta_step, axis=1)
    correction = jnp.zeros((2, SPAN, col_count), jnp.float32)
    for state_index in range(STATE):
        carried_part = (
            jnp.exp(running_delta * decay_rates[state_index][None, None, :])
            * start_state[:, state_index][:, None, :]
        )
        correction = (
            correction + mixers_blocks[:, :, STATE + state_index][:, :, None] * carried_part
        )
    ssm_out = (
        (token_major(scanned) + correction + skip_gain[None, None, :] * driven)
        .astype(jnp.bfloat16)
        .reshape(2 * SPAN, col_count)
    )
    returned = lax.all_to_all(ssm_out, "ulys", split_axis=0, concat_axis=1, tiled=True)
    mamba_output = (
        returned.astype(jnp.float32) * jax.nn.silu(gate_input.astype(jnp.float32))
    ).astype(jnp.bfloat16)
    query_local = lax.all_to_all(queries, "ulys", split_axis=1, concat_axis=0, tiled=True)
    ulys_count = lax.axis_size("ulys")
    kv_count = key_rows.shape[1] // HD
    repeat_count = ulys_count // kv_count

    def head_spread(rows_in):
        row_count = rows_in.shape[0]
        widened = jnp.broadcast_to(
            rows_in.reshape(row_count, kv_count, 1, HD), (row_count, kv_count, repeat_count, HD)
        )
        return widened.reshape(row_count, ulys_count * HD)

    key_local, value_local = (
        lax.all_to_all(head_spread(key_rows), "ulys", split_axis=1, concat_axis=0, tiled=True),
        lax.all_to_all(head_spread(value_rows), "ulys", split_axis=1, concat_axis=0, tiled=True),
    )
    heads_here = query_local.shape[1] // HD
    query_four = query_local.reshape(2, SPAN, heads_here, HD)
    query_pos = my_blocks[:, None] * SPAN + jnp.arange(SPAN, dtype=jnp.int32)[None, :]
    score_scale = HD ** (-0.5)
    initial = (
        jnp.full((2, heads_here, SPAN), NEG_LARGE, jnp.float32),
        jnp.zeros((2, heads_here, SPAN), jnp.float32),
        jnp.zeros((2, heads_here, SPAN, HD), jnp.float32),
    )
    carried = initial
    key_piece = lax.all_gather(key_local, "blk", axis=0, tiled=True)
    value_piece = lax.all_gather(value_local, "blk", axis=0, tiled=True)
    piece_rows = key_piece.shape[0]
    block_rows = SPAN
    block_count = piece_rows // block_rows
    first_rows = jnp.arange(block_count, dtype=jnp.int32) * block_rows

    def absorb_block(inner_state, block_item):
        key_block, value_block, first_row = block_item
        key_pos = row_offsets(first_row + jnp.arange(block_rows, dtype=jnp.int32), span_order)
        updated = []
        for query_side in range(2):
            side_state = (
                inner_state[0][query_side],
                inner_state[1][query_side],
                inner_state[2][query_side],
            )

            def take_block(carry_in):
                return absorb(
                    carry_in,
                    query_four[query_side],
                    query_pos[query_side],
                    key_block,
                    value_block,
                    key_pos,
                    score_scale,
                )

            def leave_block(carry_in):
                return carry_in

            side_state = lax.cond(
                jnp.min(key_pos) > query_pos[query_side, SPAN - 1],
                leave_block,
                take_block,
                side_state,
            )
            updated.append(side_state)
        merged = tuple((jnp.stack([updated[0][member], updated[1][member]]) for member in range(3)))
        return (merged, None)

    carried, _ = lax.scan(
        absorb_block,
        carried,
        (
            key_piece.reshape(block_count, block_rows, HD),
            value_piece.reshape(block_count, block_rows, HD),
            first_rows,
        ),
    )
    _, final_sum, final_acc = carried
    attended = (
        (final_acc / final_sum[..., None])
        .transpose(0, 2, 1, 3)
        .reshape(2 * SPAN, heads_here * HD)
        .astype(jnp.bfloat16)
    )
    attention_output = lax.all_to_all(attended, "ulys", split_axis=0, concat_axis=1, tiled=True)
    return (mamba_output, attention_output)


def solution(mesh):
    placed = (
        P(("blk", "ulys"), None),
        P(("blk", "ulys"), None),
        P(("blk", "ulys"), None),
        P(("blk", "ulys"), None),
        P(None, "ulys"),
        P("ulys"),
        P(None, "ulys"),
        P("ulys"),
        P(None, "ulys"),
        P("ulys"),
        P(("blk", "ulys"), None),
        P(("blk", "ulys"), None),
        P(("blk", "ulys"), None),
        P(),
    )
    return jax.shard_map(
        local,
        mesh=mesh,
        in_specs=placed,
        out_specs=(P(("blk", "ulys"), None), P(("blk", "ulys"), None)),
        check_vma=False,
    )
```

profile of v0, /device:TPU:0, one launch (start us, length us, event | category | flops | bytes accessed | tf_op | source)
XLA Modules:
  0.0 1637.5 jit_solution(13249536393559834866)
XLA Ops:
  9.5 31.8 %all_to_all.99 = bf16[256,8,128]{2,0,1:T(8,128)(2,1)} all-to-all(bf16[256,8,128]{2,0,1:T(8,128)(2,1)S(1)} %copy.142), channel_id=1, replica_groups=mesh['blk'=4,'ulys'=8] {'ulys'}, dimensions={1} | all-to-all | bytes 1048576 | tf_op jit(solution)/shard_map/all_to_all | solution.py:163
  47.1 21.6 %all_gather.23 = bf16[2048,32]{0,1:T(8,128)(2,1)S(1)} all-gather(bf16[256,32]{0,1:T(8,128)(2,1)} %param.27), channel_id=1, replica_groups=mesh['blk'=4,'ulys'=8] {'ulys'}, dimensions={0}, use_global_device_ids=true | all-gather | bytes 147456 | tf_op jit(solution)/shard_map/all_gather | solution.py:78
  74.5 11.9 copy.126
  92.7 4.4 all-to-all-start.4
  97.9 17.4 %bitcast_reduce_fusion = (f32[2,2048]{1,0:T(2,128)S(1)}, f32[2048,2048]{1,0:T(8,128)}) fusion(f32[2048]{0:T(1024)S(1)} %copy-done.51, bf16[2048,512]{1,0:T(8,128)(2,1)} %all-gather.4.cloned.1.call-done, bf16[512,2048]{1,0:T(8,128)(2,1)S(1)} %copy-done), kind=kOutput, calls=%fused_computation.268 | convolution fusion | flops 4328517632 | bytes 20996096 | tf_op jit(solution)/shard_map/dot_general | solution.py:96
  115.3 19.4 %fusion.140 = f32[2,2048,8,128]{1,2,3,0:T(8,128)} fusion(f32[2,2048,8,128]{1,3,2,0:T(8,128)} %bitcast.657), kind=kOutput, calls=%fused_computation.269 | output fusion | flops 532676608 | bytes 33554432 | tf_op jit(solution)/shard_map/reduce-window
  135.8 12.3 broadcast_add_fusion
  148.1 5.4 all-to-all-start
  153.6 10.4 all_gather.24
  165.2 17.7 %copy.136 = f32[2,2048,8,128]{1,3,2,0:T(8,128)} copy(f32[2,2048,8,128]{1,2,3,0:T(8,128)} %broadcast_add_fusion) | data formatting | bytes 33554432 | tf_op jit(solution)/shard_map/reduce_window_sum
  189.6 248.6 %while.42 = (s32[]{:T(128)}, f32[2,4,1024]{2,1,0:T(4,128)S(1)}, f32[2,4,1024]{2,1,0:T(4,128)S(1)}, f32[2,4,1024,128]{3,2,1,0:T(8,128)}, s32[8]{0:T(128)S(1)}, /*...) while((s32[]{:T(128)}, f32[2,4,1024]{2,1,0:T(4,128)S(1)}, ...), condition=%wide.region_28.29_spmd, body=%wide.region_17.28_spmd.sunk | while | flops 4392572928 | bytes 155963888 | solution.py:217
  193.4 3.9 slice_bitcast_fusion.28
  199.1 15.1 conditional.5
  199.8 4.3 fusion
  207.9 5.0 add_bitcast_fusion
  215.5 4.0 pad_maximum_fusion.9
  229.0 15.1 conditional.5
  229.7 4.3 fusion
  237.8 5.0 add_bitcast_fusion
  245.4 13.6 conditional.4
  246.1 4.2 fusion.17
  254.0 5.0 add_bitcast_fusion.2
  259.0 4.0 pad_maximum_fusion.9
  272.6 15.1 conditional.5
  273.3 4.3 fusion
  281.3 5.0 add_bitcast_fusion
  288.9 13.6 conditional.4
  289.6 4.2 fusion.17
  297.5 5.0 add_bitcast_fusion.2
  302.5 4.0 pad_maximum_fusion.9
  317.4 4.0 pad_maximum_fusion.9
  332.3 4.0 pad_maximum_fusion.9
  345.8 15.1 conditional.5
  346.5 4.3 fusion
  354.6 5.0 add_bitcast_fusion
  362.2 13.6 conditional.4
  362.8 4.2 fusion.17
  370.8 5.0 add_bitcast_fusion.2
  375.8 4.0 pad_maximum_fusion.9
  389.3 15.1 conditional.5
  390.0 4.3 fusion
  398.1 5.0 add_bitcast_fusion
  405.7 13.6 conditional.4
  406.4 4.2 fusion.17
  414.3 5.0 add_bitcast_fusion.2
  419.3 4.0 pad_maximum_fusion.9
  434.2 4.0 pad_maximum_fusion.9
  444.2 4.1 convert_element_type.124
  448.3 4.7 all-to-all-start.5
  453.0 11.4 copy.127
  465.3 9.9 all_gather.22
  475.5 11.4 bitcast_convert_fusion
  486.9 29.9 %divide_multiply_fusion = f32[2,1024,2048]{2,1,0:T(8,128)} fusion(f32[2,1024,2048]{2,1,0:T(8,128)} %bitcast_convert_fusion, f32[2,3,2048]{2,1,0:T(4,128)S(1)} %copy.129, f32[2048]{0:T(1024)S(1)} %bitcast.696, f32[2048]{0:T(1024)S(1)} %bitcast.697, f32[2048]{0:T(1024)S(1)} %bitcast.695, f32[2048]{0:T(1024)S(1)} %bitcast.694, f32[2048]{0:T(1024)S(1)} %copy-done.48), kind=kLoop, calls=%fused_computation.272 | loop fusion | flops 62914560 | bytes 33644544 | tf_op jit(solution)/shard_map/jit(silu)/mul | solution.py:94
  517.2 747.3 %while.43 = (s32[]{:T(128)}, f32[2,16,2048]{2,1,0:T(8,128)S(1)}, f32[128,8,2,2048]{3,1,0,2:T(8,128)}, f32[128,8,2,2048]{3,1,0,2:T(8,128)}, f32[16,2048]{1,0:T(8,...) while((s32[]{:T(128)}, f32[2,16,2048]{2,1,0:T(8,128)S(1)}, ...), condition=%wide.region_9.10_spmd.clone, body=%wide.region_0.9_spmd.clone.sunk | while | flops 4849674 | bytes 4005436 | solution.py:37
  1264.5 8.8 all_gather.25
  1273.4 48.9 %while.44 = (s32[]{:T(128)}, f32[16,2048]{1,0:T(8,128)S(1)}, f32[8,16,2048]{2,1,0:T(8,128)S(1)}, s32[8]{0:T(128)S(1)}, s32[8]{0:T(128)S(1)}, /*index=5*/f32[8,16...) while((s32[]{:T(128)}, f32[16,2048]{1,0:T(8,128)S(1)}, ...), condition=%wide.region_15.16_spmd.clone, body=%wide.region_14.15_spmd.clone.sunk | while | flops 131081 | bytes 786644 | solution.py:127
  1323.4 65.5 %fusion.79 = bf16[2,1024,2048]{2,1,0:T(8,128)(2,1)} fusion(f32[128,8,2,2048]{3,1,0,2:T(8,128)} %get-tuple-element.301, f32[2,2048,8,128]{1,3,2,0:T(8,128)} %copy.136, f32[2,1024,2048]{2,1,0:T(8,128)} %bitcast.660, f32[2048]{0:T(1024)S(1)} %copy-done.52, f32[2,2048]{1,0:T(2,128)S(1)} %get-tuple-element.643, f32[2048]{0:T(1024)S(1)} %bitcast.699, ...), kind=kLoop, calls=%fused_computation.188 | loop fusion | flops 281018368 | bytes 59252736 | tf_op jit(solution)/shard_map/convert_element_type | solution.py:142
  1388.8 5.1 all-to-all-start.1
  1393.9 11.9 copy.138
  1411.5 166.3 %all-to-all-done.1 = bf16[8,256,2048]{2,1,0:T(8,128)(2,1)} async-done(((bf16[8,256,2048]{2,1,0:T(8,128)(2,1)}), bf16[8,256,2048]{2,1,0:T(8,128)(2,1)}, u32[]{:S(2)}, u32[]{:S(2)}) %all-to-all-start.1) | async-done | bytes 8388640 | tf_op jit(solution)/shard_map/all_to_all | solution.py:145
  1577.9 11.3 convert_bitcast_fusion
  1589.2 16.4 %copy.137 = f32[256,8,2048]{0,2,1:T(8,128)} copy(f32[256,8,2048]{2,0,1:T(8,128)} %convert_bitcast_fusion) | data formatting | bytes 33554432 | tf_op jit(solution)/shard_map/convert_element_type | solution.py:147
  1605.6 13.3 fusion.142
  1618.9 11.9 copy.147
  (4201 shorter events, 894.1 us)
Async XLA Ops:
  7.2 90.7 %copy-start = (bf16[512,2048]{1,0:T(8,128)(2,1)S(1)}, bf16[512,2048]{1,0:T(8,128)(2,1)}, u32[]{:S(2)}) copy-start(bf16[512,2048]{1,0:T(8,128)(2,1)} %param.30) | copy-start | bytes 6291460
  7.2 84.7 %copy-start.10 = (f32[16,2048]{1,0:T(8,128)S(1)}, f32[16,2048]{1,0:T(8,128)}, u32[]{:S(2)}) copy-start(f32[16,2048]{1,0:T(8,128)} %param.32) | copy-start | bytes 393220
  7.2 90.7 %all-gather.4.cloned.1.call-start = ((), (), s32[]{:S(2)}) async-start(), calls=%async_computation.6 | async-start | bytes 2359296 | tf_op jit(solution)/shard_map/all_gather | solution.py:77
  7.9 179.2 %all-gather.8.cloned.1.call-start = ((), (), s32[]{:S(2)}) async-start(), calls=%async_computation.8 | async-start | bytes 2621440 | tf_op jit(solution)/shard_map/all_gather | solution.py:176
  41.3 56.6 %copy-start.51 = (f32[2048]{0:T(1024)S(1)}, f32[2048]{0:T(1024)}, u32[]{:S(2)}) copy-start(f32[2048]{0:T(1024)} %param.31) | copy-start | bytes 24580
  43.6 49.1 %all-to-all-start.2 = ((bf16[256,8,128]{2,0,1:T(8,128)(2,1)}), bf16[256,8,128]{2,0,1:T(8,128)(2,1)S(1)}, u32[]{:S(2)}, u32[]{:S(2)}) async-start(bf16[256,8,128]{2,0,1:T(8,128)(2,1)} %copy.140), calls=%async_computation.2 | async-start | bytes 1048576 | tf_op jit(solution)/shard_map/all_to_all | solution.py:162
  92.0 61.6 %copy-start.4 = (f32[16,2048]{1,0:T(8,128)}, f32[16,2048]{1,0:T(8,128)S(1)}, u32[]{:S(2)}) copy-start(f32[16,2048]{1,0:T(8,128)S(1)} %exponential_negate_fusion) | copy-start | bytes 393220
  92.7 55.4 %all-to-all-start.4 = ((bf16[256,8,512]{2,0,1:T(8,128)(2,1)}), bf16[256,8,512]{2,0,1:T(8,128)(2,1)}, u32[]{:S(2)}, u32[]{:S(2)}) async-start(bf16[256,8,512]{2,0,1:T(8,128)(2,1)} %bitcast.662), calls=%async_computation.4 | async-start | bytes 4194304 | tf_op jit(solution)/shard_map/all_to_all | solution.py:149
  97.1 90.0 %all-gather.6.cloned.1.call-start = ((), (), s32[]{:S(2)}) async-start(), calls=%async_computation.7 | async-start | bytes 2621440 | tf_op jit(solution)/shard_map/all_gather | solution.py:175
  148.1 300.2 %all-to-all-start = ((bf16[256,8,2048]{0,2,1:T(8,128)(2,1)}), bf16[256,8,2048]{0,2,1:T(8,128)(2,1)}, u32[]{:S(2)}, u32[]{:S(2)}) async-start(bf16[256,8,2048]{0,2,1:T(8,128)(2,1)} %bitcast.656), calls=%async_computation | async-start | bytes 16777216 | tf_op jit(solution)/shard_map/all_to_all | solution.py:75
  165.2 24.3 %copy-start.15 = (s32[8]{0:T(128)S(1)}, s32[8]{0:T(128)}, u32[]{:S(2)}) copy-start(s32[8]{0:T(128)} %param.37) | copy-start | bytes 100
  199.8 8.1 copy-start.2
  229.7 8.1 copy-start.2
  273.3 8.1 copy-start.2
  346.5 8.1 copy-start.2
  390.0 8.1 copy-start.2
  438.2 37.0 %copy-start.50 = (s32[2]{0:T(128)S(1)}, s32[2]{0:T(128)}, u32[]{:S(2)}) copy-start(s32[2]{0:T(128)} %broadcast_add_fusion.1) | copy-start | bytes 28
  448.3 940.5 %all-to-all-start.5 = ((bf16[8,256,512]{2,1,0:T(8,128)(2,1)}), bf16[8,256,512]{2,1,0:T(8,128)(2,1)}, u32[]{:S(2)}, u32[]{:S(2)}) async-start(bf16[8,256,512]{2,1,0:T(8,128)(2,1)} %convert_element_type.124), calls=%async_computation.5 | async-start | bytes 4194304 | tf_op jit(solution)/shard_map/all_to_all | solution.py:233
  464.3 22.5 %copy-start.11 = (f32[1,2048]{1,0:T(1,128)S(1)}, f32[1,2048]{1,0:T(1,128)}, u32[]{:S(2)}) copy-start(f32[1,2048]{1,0:T(1,128)} %get-tuple-element.637) | copy-start | bytes 24580
  464.3 22.5 %copy-start.12 = (f32[1,2048]{1,0:T(1,128)S(1)}, f32[1,2048]{1,0:T(1,128)}, u32[]{:S(2)}) copy-start(f32[1,2048]{1,0:T(1,128)} %get-tuple-element.638) | copy-start | bytes 24580
  464.3 22.5 %copy-start.13 = (f32[1,2048]{1,0:T(1,128)S(1)}, f32[1,2048]{1,0:T(1,128)}, u32[]{:S(2)}) copy-start(f32[1,2048]{1,0:T(1,128)} %get-tuple-element.639) | copy-start | bytes 24580
  464.4 22.5 %copy-start.14 = (f32[1,2048]{1,0:T(1,128)S(1)}, f32[1,2048]{1,0:T(1,128)}, u32[]{:S(2)}) copy-start(f32[1,2048]{1,0:T(1,128)} %get-tuple-element.640) | copy-start | bytes 24580
  464.4 22.5 %copy-start.48 = (f32[2048]{0:T(1024)S(1)}, f32[2048]{0:T(1024)}, u32[]{:S(2)}) copy-start(f32[2048]{0:T(1024)} %param.29) | copy-start | bytes 24580
  486.9 30.2 %copy-start.5 = (f32[16,2048]{1,0:T(8,128)S(1)}, f32[16,2048]{1,0:T(8,128)}, u32[]{:S(2)}) copy-start(f32[16,2048]{1,0:T(8,128)} %copy-done.4) | copy-start | bytes 393220
  486.9 30.2 %copy-start.6 = (f32[2,16,2048]{2,1,0:T(8,128)S(1)}, f32[2,16,2048]{2,1,0:T(8,128)}, u32[]{:S(2)}) copy-start(f32[2,16,2048]{2,1,0:T(8,128)} %custom-call) | copy-start | bytes 786436
  516.8 756.6 %copy-start.7 = (f32[16,2048]{1,0:T(8,128)S(1)}, f32[16,2048]{1,0:T(8,128)}, u32[]{:S(2)}) copy-start(f32[16,2048]{1,0:T(8,128)} %custom-call.1) | copy-start | bytes 393220
  516.8 756.6 %copy-start.9 = (f32[8,16,2048]{2,1,0:T(8,128)S(1)}, f32[8,16,2048]{2,1,0:T(8,128)}, u32[]{:S(2)}) copy-start(f32[8,16,2048]{2,1,0:T(8,128)} %custom-call.4) | copy-start | bytes 3145732
  516.8 756.6 %copy-start.53 = (s32[8]{0:T(128)S(1)}, s32[8]{0:T(128)}, u32[]{:S(2)}) copy-start(s32[8]{0:T(128)} %select_reduce_fusion.2) | copy-start | bytes 100
  516.8 806.2 %copy-start.16 = (f32[2,1024]{1,0:T(2,128)S(1)}, f32[2,1024]{1,0:T(2,128)}, u32[]{:S(2)}) copy-start(f32[2,1024]{1,0:T(2,128)} %get-tuple-element.587) | copy-start | bytes 24580
  516.8 806.2 %copy-start.17 = (f32[2,1024]{1,0:T(2,128)S(1)}, f32[2,1024]{1,0:T(2,128)}, u32[]{:S(2)}) copy-start(f32[2,1024]{1,0:T(2,128)} %get-tuple-element.588) | copy-start | bytes 24580
  516.8 806.2 %copy-start.18 = (f32[2,1024]{1,0:T(2,128)S(1)}, f32[2,1024]{1,0:T(2,128)}, u32[]{:S(2)}) copy-start(f32[2,1024]{1,0:T(2,128)} %get-tuple-element.589) | copy-start | bytes 24580
  516.8 806.2 %copy-start.19 = (f32[2,1024]{1,0:T(2,128)S(1)}, f32[2,1024]{1,0:T(2,128)}, u32[]{:S(2)}) copy-start(f32[2,1024]{1,0:T(2,128)} %get-tuple-element.590) | copy-start | bytes 24580
  516.8 806.2 %copy-start.20 = (f32[2,1024]{1,0:T(2,128)S(1)}, f32[2,1024]{1,0:T(2,128)}, u32[]{:S(2)}) copy-start(f32[2,1024]{1,0:T(2,128)} %get-tuple-element.591) | copy-start | bytes 24580
  516.8 806.2 %copy-start.21 = (f32[2,1024]{1,0:T(2,128)S(1)}, f32[2,1024]{1,0:T(2,128)}, u32[]{:S(2)}) copy-start(f32[2,1024]{1,0:T(2,128)} %get-tuple-element.592) | copy-start | bytes 24580
  516.8 806.2 %copy-start.22 = (f32[2,1024]{1,0:T(2,128)S(1)}, f32[2,1024]{1,0:T(2,128)}, u32[]{:S(2)}) copy-start(f32[2,1024]{1,0:T(2,128)} %get-tuple-element.593) | copy-start | bytes 24580
  516.9 806.2 %copy-start.23 = (f32[2,1024]{1,0:T(2,128)S(1)}, f32[2,1024]{1,0:T(2,128)}, u32[]{:S(2)}) copy-start(f32[2,1024]{1,0:T(2,128)} %get-tuple-element.594) | copy-start | bytes 24580
  516.9 806.2 %copy-start.24 = (f32[2,1024]{1,0:T(2,128)S(1)}, f32[2,1024]{1,0:T(2,128)}, u32[]{:S(2)}) copy-start(f32[2,1024]{1,0:T(2,128)} %get-tuple-element.595) | copy-start | bytes 24580
  516.9 806.2 %copy-start.25 = (f32[2,1024]{1,0:T(2,128)S(1)}, f32[2,1024]{1,0:T(2,128)}, u32[]{:S(2)}) copy-start(f32[2,1024]{1,0:T(2,128)} %get-tuple-element.596) | copy-start | bytes 24580
  516.9 806.2 %copy-start.26 = (f32[2,1024]{1,0:T(2,128)S(1)}, f32[2,1024]{1,0:T(2,128)}, u32[]{:S(2)}) copy-start(f32[2,1024]{1,0:T(2,128)} %get-tuple-element.597) | copy-start | bytes 24580
  516.9 806.2 %copy-start.27 = (f32[2,1024]{1,0:T(2,128)S(1)}, f32[2,1024]{1,0:T(2,128)}, u32[]{:S(2)}) copy-start(f32[2,1024]{1,0:T(2,128)} %get-tuple-element.598) | copy-start | bytes 24580
  516.9 806.2 %copy-start.28 = (f32[2,1024]{1,0:T(2,128)S(1)}, f32[2,1024]{1,0:T(2,128)}, u32[]{:S(2)}) copy-start(f32[2,1024]{1,0:T(2,128)} %get-tuple-element.599) | copy-start | bytes 24580
  516.9 806.2 %copy-start.29 = (f32[2,1024]{1,0:T(2,128)S(1)}, f32[2,1024]{1,0:T(2,128)}, u32[]{:S(2)}) copy-start(f32[2,1024]{1,0:T(2,128)} %get-tuple-element.600) | copy-start | bytes 24580
  516.9 806.2 %copy-start.30 = (f32[2,1024]{1,0:T(2,128)S(1)}, f32[2,1024]{1,0:T(2,128)}, u32[]{:S(2)}) copy-start(f32[2,1024]{1,0:T(2,128)} %get-tuple-element.601) | copy-start | bytes 24580
  516.9 806.2 %copy-start.31 = (f32[2,1024]{1,0:T(2,128)S(1)}, f32[2,1024]{1,0:T(2,128)}, u32[]{:S(2)}) copy-start(f32[2,1024]{1,0:T(2,128)} %get-tuple-element.602) | copy-start | bytes 24580
  516.9 806.2 %copy-start.32 = (f32[1,2048]{1,0:T(1,128)S(1)}, f32[1,2048]{1,0:T(1,128)}, u32[]{:S(2)}) copy-start(f32[1,2048]{1,0:T(1,128)} %get-tuple-element.621) | copy-start | bytes 24580
  517.0 806.2 %copy-start.33 = (f32[1,2048]{1,0:T(1,128)S(1)}, f32[1,2048]{1,0:T(1,128)}, u32[]{:S(2)}) copy-start(f32[1,2048]{1,0:T(1,128)} %get-tuple-element.622) | copy-start | bytes 24580
  517.0 806.2 %copy-start.34 = (f32[1,2048]{1,0:T(1,128)S(1)}, f32[1,2048]{1,0:T(1,128)}, u32[]{:S(2)}) copy-start(f32[1,2048]{1,0:T(1,128)} %get-tuple-element.623) | copy-start | bytes 24580
  517.0 806.2 %copy-start.35 = (f32[1,2048]{1,0:T(1,128)S(1)}, f32[1,2048]{1,0:T(1,128)}, u32[]{:S(2)}) copy-start(f32[1,2048]{1,0:T(1,128)} %get-tuple-element.624) | copy-start | bytes 24580
  517.0 806.2 %copy-start.36 = (f32[1,2048]{1,0:T(1,128)S(1)}, f32[1,2048]{1,0:T(1,128)}, u32[]{:S(2)}) copy-start(f32[1,2048]{1,0:T(1,128)} %get-tuple-element.625) | copy-start | bytes 24580
  517.0 806.2 %copy-start.37 = (f32[1,2048]{1,0:T(1,128)S(1)}, f32[1,2048]{1,0:T(1,128)}, u32[]{:S(2)}) copy-start(f32[1,2048]{1,0:T(1,128)} %get-tuple-element.626) | copy-start | bytes 24580
  517.0 806.2 %copy-start.38 = (f32[1,2048]{1,0:T(1,128)S(1)}, f32[1,2048]{1,0:T(1,128)}, u32[]{:S(2)}) copy-start(f32[1,2048]{1,0:T(1,128)} %get-tuple-element.627) | copy-start | bytes 24580
  517.0 806.2 %copy-start.39 = (f32[1,2048]{1,0:T(1,128)S(1)}, f32[1,2048]{1,0:T(1,128)}, u32[]{:S(2)}) copy-start(f32[1,2048]{1,0:T(1,128)} %get-tuple-element.628) | copy-start | bytes 24580
  517.0 806.2 %copy-start.40 = (f32[1,2048]{1,0:T(1,128)S(1)}, f32[1,2048]{1,0:T(1,128)}, u32[]{:S(2)}) copy-start(f32[1,2048]{1,0:T(1,128)} %get-tuple-element.629) | copy-start | bytes 24580
  517.0 806.2 %copy-start.41 = (f32[1,2048]{1,0:T(1,128)S(1)}, f32[1,2048]{1,0:T(1,128)}, u32[]{:S(2)}) copy-start(f32[1,2048]{1,0:T(1,128)} %get-tuple-element.630) | copy-start | bytes 24580
  517.0 806.2 %copy-start.42 = (f32[1,2048]{1,0:T(1,128)S(1)}, f32[1,2048]{1,0:T(1,128)}, u32[]{:S(2)}) copy-start(f32[1,2048]{1,0:T(1,128)} %get-tuple-element.631) | copy-start | bytes 24580
  517.1 806.2 %copy-start.43 = (f32[1,2048]{1,0:T(1,128)S(1)}, f32[1,2048]{1,0:T(1,128)}, u32[]{:S(2)}) copy-start(f32[1,2048]{1,0:T(1,128)} %get-tuple-element.632) | copy-start | bytes 24580
  517.1 806.2 %copy-start.44 = (f32[1,2048]{1,0:T(1,128)S(1)}, f32[1,2048]{1,0:T(1,128)}, u32[]{:S(2)}) copy-start(f32[1,2048]{1,0:T(1,128)} %get-tuple-element.633) | copy-start | bytes 24580
  517.1 806.2 %copy-start.45 = (f32[1,2048]{1,0:T(1,128)S(1)}, f32[1,2048]{1,0:T(1,128)}, u32[]{:S(2)}) copy-start(f32[1,2048]{1,0:T(1,128)} %get-tuple-element.634) | copy-start | bytes 24580
  517.1 806.2 %copy-start.46 = (f32[1,2048]{1,0:T(1,128)S(1)}, f32[1,2048]{1,0:T(1,128)}, u32[]{:S(2)}) copy-start(f32[1,2048]{1,0:T(1,128)} %get-tuple-element.635) | copy-start | bytes 24580
  517.1 806.2 %copy-start.47 = (f32[1,2048]{1,0:T(1,128)S(1)}, f32[1,2048]{1,0:T(1,128)}, u32[]{:S(2)}) copy-start(f32[1,2048]{1,0:T(1,128)} %get-tuple-element.636) | copy-start | bytes 24580
  517.1 805.2 %copy-start.49 = (pred[2,8]{1,0:T(4,128)(4,1)S(1)}, pred[2,8]{1,0:T(4,128)(4,1)}, u32[]{:S(2)}) copy-start(pred[2,8]{1,0:T(4,128)(4,1)} %iota_compare_fusion.2) | copy-start | bytes 52
  517.1 806.2 %copy-start.52 = (f32[2048]{0:T(1024)S(1)}, f32[2048]{0:T(1024)}, u32[]{:S(2)}) copy-start(f32[2048]{0:T(1024)} %param.33) | copy-start | bytes 24580
  1388.8 189.1 %all-to-all-start.1 = ((bf16[8,256,2048]{2,1,0:T(8,128)(2,1)}), bf16[8,256,2048]{2,1,0:T(8,128)(2,1)}, u32[]{:S(2)}, u32[]{:S(2)}) async-start(bf16[8,256,2048]{2,1,0:T(8,128)(2,1)} %bitcast.661), calls=%async_computation.1 | async-start | bytes 16777216 | tf_op jit(solution)/shard_map/all_to_all | solution.py:145
  1605.6 25.2 %copy-start.1 = (bf16[512,2048]{1,0:T(8,128)(2,1)S(1)}, bf16[512,2048]{1,0:T(8,128)(2,1)}, u32[]{:S(2)}) copy-start(bf16[512,2048]{1,0:T(8,128)(2,1)} %param.30) | copy-start | bytes 6291460
  (6 other events, 11.3 us)
Sparse Core Ops, SparseCore 0:
  9.6 39.6 all-gather.3
  51.2 33.8 all-gather.7
  99.8 36.5 all-gather.5
where the time goes:
time: 1650 us; the launch traced here: 1640 us
  local copies, waits for them, and re-layouts  703 us (43%)
  other arithmetic  470 us (28%)
  waiting for transfers between devices  168 us (10%)
  matrix products  101 us (6%)
  blocking collectives  82.6 us (5%)
  loops' own time  75.2 us (5%)
  starting transfers between devices  23.4 us (1%)
    slice x128, local copies, waits for them, and re-layouts, token_scan(): return lax.scan(advance, start_state, steps_in, unroll=8)  312 us
    reduce_sum x384, other arithmetic, advance(): return (hidden, jnp.sum(readout_now[:, :, None] * hidden, axis=1))  185 us
    all_to_all x1, waiting for transfers between devices, local(): lax.all_to_all(ssm_out, 'ulys', split_axis=0, concat_axis=1, tiled=True)  166 us
    mul x128, local copies, waits for them, and re-layouts, advance(): (delta_now * driven_now)[:, None, :] * inject_now[:, :, None]  98 us
    dynamic_update_slice x128, local copies, waits for them, and re-layouts, token_scan(): return lax.scan(advance, start_state, steps_in, unroll=8)  94.4 us
    convert_element_type x1, other arithmetic, local(): ssm_out = (token_major(scanned) + correction + skip_gain[None, None, :] *...  65.5 us
    dot_general x9, matrix products, absorb(): jnp.einsum('hqk,kd->hqd', weights.astype(jnp.bfloat16), value_block, pref...  45 us
    unnamed x118, local copies, waits for them, and re-layouts  41.4 us

commit v1 on v0

v1 whole, which is shorter than its diff:
```python
import functools

import jax
import jax.numpy as jnp
from jax import lax
from jax.experimental import pallas as pl
from jax.experimental.pallas import tpu as pltpu
from jax.sharding import Mesh
from jax.sharding import PartitionSpec as P

STATE = 16
CONV = 4
HD = 128
SPAN = 1024
LANES = 128
PAIR = 2
GROUP = 16
NEG_LARGE = -1e30
LOG2E = 1.4426950408889634
PARAM_ROWS = 24
VMEM_LIMIT = 56 * 1024 * 1024


def softplus(x):
    e = jnp.exp(-jnp.abs(x))
    return jnp.maximum(x, 0.0) + jnp.log1p(e)


def scan_kernel(
    core_ref, own_ref, other_ref, halo_ref, low_ref, weight_ref, param_ref, inject_ref, read_ref,
    delta_ref, y_ref, end_ref, total_ref,
    x_scr, driven_scr, push_scr, hist_scr,
):
    core = core_ref[0]
    tokens, cols = delta_ref.shape
    half = tokens // 2
    depth = low_ref.shape[1]
    x_scr[0:8, :] = halo_ref[...].astype(jnp.float32)
    x_scr[pl.ds(pl.multiple_of(8 + core * half, 8), half), :] = own_ref[...].astype(jnp.float32)
    x_scr[pl.ds(pl.multiple_of(8 + (1 - core) * half, 8), half), :] = other_ref[...].astype(jnp.float32)
    params = param_ref[0]
    weight = weight_ref[...].reshape(depth, cols)
    delta_ref[...] = jnp.dot(low_ref[...], weight, preferred_element_type=jnp.float32)
    rows = 16
    taps = [params[STATE + k : STATE + k + 1, :] for k in range(CONV)]
    conv_bias = params[STATE + CONV : STATE + CONV + 1, :]
    delta_bias = params[STATE + CONV + 1 : STATE + CONV + 2, :]
    skip = params[STATE + CONV + 2 : STATE + CONV + 3, :]

    def prepare(step, carry):
        first = pl.multiple_of(step * rows, rows)
        window = x_scr[pl.ds(first, rows + 8), :]
        mixed = jnp.broadcast_to(conv_bias, (rows, cols))
        for k in range(CONV):
            lo = 8 - (CONV - 1) + k
            mixed = mixed + taps[k] * window[lo : lo + rows, :]
        driven = mixed * jax.nn.sigmoid(mixed)
        delta = softplus(delta_ref[pl.ds(first, rows), :] + delta_bias)
        delta_ref[pl.ds(first, rows), :] = delta
        driven_scr[pl.ds(first, rows), :] = driven * skip
        push_scr[pl.ds(first, rows), :] = driven * delta
        return carry + delta.reshape(rows // 8, 8, cols).sum(axis=0)

    total = lax.fori_loop(0, tokens // rows, prepare, jnp.zeros((8, cols), jnp.float32))
    total_ref[...] = jnp.broadcast_to(jnp.sum(total, axis=0, keepdims=True), (8, cols))
    rates = -LOG2E * jnp.exp(params[:STATE, :])
    reps = cols // LANES

    def step16(group, hidden):
        base = pl.multiple_of(group * GROUP, GROUP)
        for i in range(GROUP):
            delta = delta_ref[pl.ds(base + i, 1), :]
            push = push_scr[pl.ds(base + i, 1), :]
            inject = inject_ref[pl.ds(pl.multiple_of((base + i) * STATE, STATE), STATE), :]
            inject = jnp.concatenate([inject] * reps, axis=1)
            hidden = jnp.exp2(delta * rates) * hidden + push * inject
            hist_scr[i * STATE : (i + 1) * STATE, :] = hidden.astype(jnp.bfloat16)
        read = read_ref[pl.ds(base, GROUP), :]
        out = jnp.dot(read, hist_scr[...], preferred_element_type=jnp.float32)
        y_ref[pl.ds(base, GROUP), :] = (out + driven_scr[pl.ds(base, GROUP), :]).astype(y_ref.dtype)
        return hidden

    end_ref[...] = lax.fori_loop(
        0, tokens // GROUP, step16, jnp.zeros((STATE, cols), jnp.float32)
    )


def correct_kernel(
    core_ref, delta_ref, y_ref, enter_ref, param_ref, read_ref, own_gate_ref, other_gate_ref,
    mine_ref, theirs_ref, hist_scr, out_scr,
):
    core = core_ref[0]
    tokens, cols = delta_ref.shape
    half = tokens // 2
    rates = -LOG2E * jnp.exp(param_ref[0][:STATE, :])
    enter = enter_ref[...].astype(jnp.float32)

    def step16(group, elapsed):
        base = pl.multiple_of(group * GROUP, GROUP)
        for i in range(GROUP):
            elapsed = elapsed + delta_ref[pl.ds(base + i, 1), :]
            carried = jnp.exp2(elapsed * rates) * enter
            hist_scr[i * STATE : (i + 1) * STATE, :] = carried.astype(jnp.bfloat16)
        read = read_ref[pl.ds(base, GROUP), :]
        out = jnp.dot(read, hist_scr[...], preferred_element_type=jnp.float32)
        total = out + y_ref[pl.ds(base, GROUP), :].astype(jnp.float32)
        out_scr[pl.ds(base, GROUP), :] = total.astype(jnp.bfloat16).astype(jnp.float32)
        return elapsed

    lax.fori_loop(0, tokens // GROUP, step16, jnp.zeros((1, cols), jnp.float32))
    rows = 16

    def gated(gate_ref, dest_ref, offset):
        def body(step, carry):
            first = pl.multiple_of(step * rows, rows)
            gate = gate_ref[pl.ds(first, rows), :].astype(jnp.float32)
            value = out_scr[pl.ds(pl.multiple_of(offset + first, 8), rows), :]
            dest_ref[pl.ds(first, rows), :] = (
                value * (gate * jax.nn.sigmoid(gate))
            ).astype(dest_ref.dtype)
            return carry

        lax.fori_loop(0, half // rows, body, 0)

    gated(own_gate_ref, mine_ref, core * half)
    gated(other_gate_ref, theirs_ref, (1 - core) * half)


def combine_kernel(order_ref, end_ref, total_ref, rate_ref, enter_ref):
    chunks = end_ref.shape[0]
    rates = rate_ref[...]

    def body(place, state):
        chunk = order_ref[place]
        enter_ref[chunk] = state.astype(enter_ref.dtype)
        total = total_ref[chunk]
        return jnp.exp2(total[0:1, :] * rates) * state + end_ref[chunk]

    lax.fori_loop(0, chunks, body, jnp.zeros(rates.shape, jnp.float32))


def flash_kernel(
    side_ref, block_ref, diag_ref, first_ref, last_ref, q_ref, kv_ref, out_ref,
    max_scr, acc_scr, value_scr, *, heads, rows,
):
    step = pl.program_id(0)
    scale = LOG2E * HD ** (-0.5)
    span = kv_ref.shape[0]
    value_scr[:, :HD] = kv_ref[:, HD:]
    value_scr[:, HD:] = jnp.ones((span, HD), jnp.bfloat16)

    @pl.when(first_ref[step] == 1)
    def _():
        max_scr[...] = jnp.full(max_scr.shape, NEG_LARGE, jnp.float32)
        acc_scr[...] = jnp.zeros(acc_scr.shape, jnp.float32)

    def absorb(head, row, key_count, masked):
        q = q_ref[row : row + rows, head * HD : (head + 1) * HD]
        scores = lax.dot_general(
            q, kv_ref[:key_count, :HD], (((1,), (1,)), ((), ())),
            preferred_element_type=jnp.float32,
        ) * scale
        if masked:
            query_at = lax.broadcasted_iota(jnp.int32, scores.shape, 0) + row
            key_at = lax.broadcasted_iota(jnp.int32, scores.shape, 1)
            scores = jnp.where(key_at <= query_at, scores, NEG_LARGE)
        at = slice(head * span + row, head * span + row + rows)
        old_max = max_scr[at, :]
        new_max = jnp.maximum(old_max, jnp.max(scores, axis=1, keepdims=True))
        weights = jnp.exp2(scores - new_max[:, :1]).astype(jnp.bfloat16)
        shrink = jnp.exp2(old_max - new_max)
        acc_scr[at, :] = acc_scr[at, :] * shrink[:, :1] + jnp.dot(
            weights, value_scr[:key_count, :], preferred_element_type=jnp.float32
        )
        max_scr[at, :] = new_max

    @pl.when(diag_ref[step] == 0)
    def _():
        for head in range(heads):
            for row in range(0, span, rows):
                absorb(head, row, span, False)

    @pl.when(diag_ref[step] == 1)
    def _():
        for head in range(heads):
            for row in range(0, span, rows):
                absorb(head, row, row + rows, True)

    @pl.when(last_ref[step] == 1)
    def _():
        for head in range(heads):
            for row in range(0, span, rows):
                at = slice(head * span + row, head * span + row + rows)
                out_ref[row : row + rows, head * HD : (head + 1) * HD] = (
                    acc_scr[at, :HD] / acc_scr[at, HD:]
                ).astype(out_ref.dtype)


def run_scan(core, x_own, x_other, halo, low, weight, params, inject, read, col_block):
    half, _ = x_own.shape
    tokens = 2 * half
    cols = x_other.shape[1]
    shard_cols = params.shape[2]
    per_shard = shard_cols // col_block
    parts, _, part_rows, _ = weight.shape
    blocks = cols // col_block

    def own_map(j, core_ref):
        return (0, (PAIR * (j // per_shard) + core_ref[0]) * per_shard + j % per_shard)

    def plain(j, core_ref):
        return (0, j)

    def fixed(j, core_ref):
        return (0, 0)

    grid_spec = pltpu.PrefetchScalarGridSpec(
        num_scalar_prefetch=1,
        grid=(blocks,),
        in_specs=[
            pl.BlockSpec((half, col_block), own_map),
            pl.BlockSpec((half, col_block), plain),
            pl.BlockSpec((8, col_block), plain),
            pl.BlockSpec(low.shape, fixed, pipeline_mode=pl.Buffered(1)),
            pl.BlockSpec(
                (parts, 1, part_rows, col_block),
                lambda j, core_ref: (0, j // per_shard, 0, j % per_shard),
            ),
            pl.BlockSpec(
                (1, PARAM_ROWS, col_block),
                lambda j, core_ref: (j // per_shard, 0, j % per_shard),
            ),
            pl.BlockSpec(inject.shape, fixed, pipeline_mode=pl.Buffered(1)),
            pl.BlockSpec(read.shape, fixed, pipeline_mode=pl.Buffered(1)),
        ],
        out_specs=[
            pl.BlockSpec((tokens, col_block), plain),
            pl.BlockSpec((tokens, col_block), plain),
            pl.BlockSpec((STATE, col_block), plain),
            pl.BlockSpec((8, col_block), plain),
        ],
        scratch_shapes=[
            pltpu.VMEM((tokens + 8, col_block), jnp.float32),
            pltpu.VMEM((tokens, col_block), jnp.float32),
            pltpu.VMEM((tokens, col_block), jnp.float32),
            pltpu.VMEM((GROUP * STATE, col_block), jnp.bfloat16),
        ],
    )
    return pl.pallas_call(
        scan_kernel,
        grid_spec=grid_spec,
        out_shape=[
            jax.ShapeDtypeStruct((tokens, cols), jnp.float32),
            jax.ShapeDtypeStruct((tokens, cols), jnp.bfloat16),
            jax.ShapeDtypeStruct((STATE, cols), jnp.float32),
            jax.ShapeDtypeStruct((8, cols), jnp.float32),
        ],
        compiler_params=pltpu.CompilerParams(vmem_limit_bytes=VMEM_LIMIT),
        name="token_scan",
    )(core, x_own, x_other, halo, low, weight, params, inject, read)


def run_correct(core, delta, y, enter, params, read, gate_own, gate_other, col_block):
    tokens, cols = delta.shape
    half = tokens // 2
    shard_cols = params.shape[2]
    per_shard = shard_cols // col_block
    blocks = cols // col_block

    def own_map(j, core_ref):
        return (0, (PAIR * (j // per_shard) + core_ref[0]) * per_shard + j % per_shard)

    def plain(j, core_ref):
        return (0, j)

    grid_spec = pltpu.PrefetchScalarGridSpec(
        num_scalar_prefetch=1,
        grid=(blocks,),
        in_specs=[
            pl.BlockSpec((tokens, col_block), plain),
            pl.BlockSpec((tokens, col_block), plain),
            pl.BlockSpec((STATE, col_block), plain),
            pl.BlockSpec(
                (1, PARAM_ROWS, col_block),
                lambda j, core_ref: (j // per_shard, 0, j % per_shard),
            ),
            pl.BlockSpec(read.shape, lambda j, core_ref: (0, 0), pipeline_mode=pl.Buffered(1)),
            pl.BlockSpec((half, col_block), own_map),
            pl.BlockSpec((half, col_block), plain),
        ],
        out_specs=[
            pl.BlockSpec((half, col_block), plain),
            pl.BlockSpec((half, col_block), plain),
        ],
        scratch_shapes=[
            pltpu.VMEM((GROUP * STATE, col_block), jnp.bfloat16),
            pltpu.VMEM((tokens, col_block), jnp.float32),
        ],
    )
    return pl.pallas_call(
        correct_kernel,
        grid_spec=grid_spec,
        out_shape=[jax.ShapeDtypeStruct((half, cols), jnp.bfloat16)] * 2,
        compiler_params=pltpu.CompilerParams(vmem_limit_bytes=VMEM_LIMIT),
        name="state_correction",
    )(core, delta, y, enter, params, read, gate_own, gate_other)


def run_combine(order, ends, totals, rates):
    chunks, _, cols = ends.shape
    return pl.pallas_call(
        combine_kernel,
        grid_spec=pltpu.PrefetchScalarGridSpec(
            num_scalar_prefetch=1,
            grid=(1,),
            in_specs=[
                pl.BlockSpec(ends.shape, lambda i, o: (0, 0, 0)),
                pl.BlockSpec(totals.shape, lambda i, o: (0, 0, 0)),
                pl.BlockSpec(rates.shape, lambda i, o: (0, 0)),
            ],
            out_specs=pl.BlockSpec(ends.shape, lambda i, o: (0, 0, 0)),
        ),
        out_shape=jax.ShapeDtypeStruct(ends.shape, jnp.bfloat16),
        compiler_params=pltpu.CompilerParams(vmem_limit_bytes=VMEM_LIMIT),
        name="state_combine",
    )(order, ends, totals, rates)


def run_flash(tables, q, kv, rows=512):
    tokens, width = q.shape
    heads = width // HD
    steps = tables[0].shape[0]

    def q_map(s, side, block, diag, first, last):
        return (side[s], 0)

    def kv_map(s, side, block, diag, first, last):
        return (block[s], 0)

    return pl.pallas_call(
        functools.partial(flash_kernel, heads=heads, rows=rows),
        grid_spec=pltpu.PrefetchScalarGridSpec(
            num_scalar_prefetch=5,
            grid=(steps,),
            in_specs=[pl.BlockSpec((SPAN, width), q_map), pl.BlockSpec((SPAN, 2 * HD), kv_map)],
            out_specs=pl.BlockSpec((SPAN, width), q_map),
            scratch_shapes=[
                pltpu.VMEM((heads * SPAN, HD), jnp.float32),
                pltpu.VMEM((heads * SPAN, 2 * HD), jnp.float32),
                pltpu.VMEM((SPAN, 2 * HD), jnp.bfloat16),
            ],
        ),
        out_shape=jax.ShapeDtypeStruct(q.shape, jnp.bfloat16),
        compiler_params=pltpu.CompilerParams(vmem_limit_bytes=VMEM_LIMIT),
        name="causal_attention",
    )(*tables, q, kv)


def flash_tables(span_order, my_blocks):
    block_total = span_order.shape[0]
    places = jnp.arange(block_total, dtype=jnp.int32)
    holder = jnp.sum(jnp.where(span_order[None, :] == places[:, None], places[None, :], 0), axis=1)
    steps = jnp.arange(block_total + 1, dtype=jnp.int32)
    first_count = my_blocks[0] + 1
    side = (steps >= first_count).astype(jnp.int32)
    place = jnp.where(side == 1, steps - first_count, steps)
    limit = jnp.where(side == 1, my_blocks[1], my_blocks[0])
    block = jnp.sum(jnp.where(places[None, :] == place[:, None], holder[None, :], 0), axis=1)
    last = (place == limit).astype(jnp.int32)
    first = (place == 0).astype(jnp.int32)
    return (side, block.astype(jnp.int32), last, first, last)


def local(
    mamba_input, gate_input, delta_low, state_mixers, conv_weight, conv_bias, delta_weight,
    delta_bias, decay_log, skip_gain, queries, key_rows, value_rows, span_order,
):
    blk = lax.axis_index("blk")
    chip = lax.axis_index("chip")
    core = lax.axis_index("core")
    blk_count = lax.axis_size("blk")
    chip_count = lax.axis_size("chip")
    ulys = ("chip", "core")
    ulys_count = chip_count * PAIR
    chunks = blk_count * chip_count
    block_total = span_order.shape[0]
    half, inner = mamba_input.shape
    tokens = PAIR * half
    shard_cols = delta_weight.shape[1]
    cols = inner // PAIR
    col_block = min(1024, shard_cols)
    swap = [(0, 1), (1, 0)]
    core_arr = core.astype(jnp.int32).reshape(1)
    my_blocks = lax.dynamic_slice_in_dim(span_order, 2 * blk, 2, 0)

    kv_heads = key_rows.shape[1] // HD
    repeat = ulys_count // kv_heads
    kv_rows = jnp.stack(
        [key_rows.reshape(half, kv_heads, HD), value_rows.reshape(half, kv_heads, HD)], axis=2
    )
    kv_rows = jnp.broadcast_to(
        kv_rows[:, :, None], (half, kv_heads, repeat, 2, HD)
    ).reshape(half, ulys_count * 2 * HD)
    kv_local = lax.all_to_all(kv_rows, ulys, split_axis=1, concat_axis=0, tiled=True)
    kv_all = lax.all_gather(kv_local, "blk", axis=0, tiled=True)
    q_local = lax.all_to_all(queries, ulys, split_axis=1, concat_axis=0, tiled=True)

    depth = delta_weight.shape[0]
    part_rows = depth // blk_count
    part = lax.dynamic_slice_in_dim(delta_weight, blk * part_rows, part_rows, 0)
    weight = lax.all_gather(part, ("blk", "chip"), axis=0, tiled=False)
    weight = weight.reshape(blk_count, chip_count, part_rows, shard_cols)
    packed = jnp.concatenate(
        [
            decay_log,
            conv_weight.astype(jnp.float32),
            conv_bias[None],
            delta_bias[None],
            skip_gain[None],
            jnp.zeros((1, shard_cols), jnp.float32),
        ],
        axis=0,
    )
    params = lax.all_gather(packed, "chip", axis=0, tiled=False)

    def other_half(array):
        parts = array.reshape(half, chip_count, PAIR, shard_cols)
        picked = lax.dynamic_index_in_dim(parts, 1 - core, 2, False)
        return picked.reshape(half, cols)

    x_other = lax.ppermute(other_half(mamba_input), "core", swap)
    gate_other = lax.ppermute(other_half(gate_input), "core", swap)
    low = lax.all_gather(delta_low, "core", axis=0, tiled=True)
    mixers = lax.all_gather(state_mixers, "core", axis=0, tiled=True)
    inject = jnp.broadcast_to(
        mixers[:, :STATE].astype(jnp.float32).reshape(tokens * STATE, 1), (tokens * STATE, LANES)
    )
    same = jnp.arange(tokens, dtype=jnp.int32)[:, None] % GROUP == jnp.arange(GROUP, dtype=jnp.int32)
    read = jnp.where(
        same[:, :, None], mixers[:, None, STATE:], jnp.zeros((), jnp.bfloat16)
    ).reshape(tokens, GROUP * STATE)

    per_block = SPAN // tokens
    chunk_ids = jnp.arange(chunks, dtype=jnp.int32)
    stored = chunk_ids // per_block
    block_ids = jnp.arange(block_total, dtype=jnp.int32)
    block_pos = jnp.sum(
        jnp.where(stored[:, None] == block_ids[None, :], span_order[None, :], 0), axis=1
    )
    chunk_pos = block_pos * per_block + chunk_ids % per_block
    order = jnp.sum(
        jnp.where(chunk_pos[None, :] == chunk_ids[:, None], chunk_ids[None, :], 0), axis=1
    ).astype(jnp.int32)
    me = blk * chip_count + chip
    my_pos = jnp.sum(jnp.where(chunk_ids == me, chunk_pos, 0))
    own_cols = lax.dynamic_index_in_dim(
        mamba_input[half - 8 :].reshape(8, chip_count, PAIR, shard_cols), core, 2, False
    ).reshape(8, cols)
    tail = jnp.where(core == 1, own_cols, x_other[half - 8 :])
    tails = lax.all_to_all(
        jnp.broadcast_to(tail[None, 8 - (CONV - 1) :], (chunks, CONV - 1, cols)),
        ("blk", "chip"), split_axis=0, concat_axis=0, tiled=True,
    )
    before = (chunk_pos == my_pos - 1).astype(jnp.bfloat16)
    halo = jnp.einsum("m,mkc->kc", before, tails, preferred_element_type=jnp.float32)
    halo = jnp.concatenate(
        [jnp.zeros((8 - (CONV - 1), cols), jnp.bfloat16), halo.astype(jnp.bfloat16)], axis=0
    )

    delta, y_local, ends, totals = run_scan(
        core_arr, mamba_input, x_other, halo, low, weight, params, inject, read, col_block
    )

    piece = cols // chunks
    top = totals[0:1]
    hi = top.astype(jnp.bfloat16)
    rest = top - hi.astype(jnp.float32)
    mid = rest.astype(jnp.bfloat16)
    tiny = (rest - mid.astype(jnp.float32)).astype(jnp.bfloat16)
    sent = jnp.concatenate([ends.astype(jnp.bfloat16), hi, mid, tiny], axis=0)
    sent_rows = STATE + 3
    got = lax.all_to_all(
        sent.reshape(sent_rows, chunks, piece).transpose(1, 0, 2), ("blk", "chip"),
        split_axis=0, concat_axis=0, tiled=True,
    ).astype(jnp.float32)
    got_totals = jnp.sum(got[:, STATE:], axis=1, keepdims=True)
    rates = -LOG2E * jnp.exp(params[:, :STATE].transpose(1, 0, 2).reshape(STATE, cols))
    my_rates = lax.dynamic_slice_in_dim(rates, me * piece, piece, 1)
    enter = run_combine(order, got[:, :STATE], got_totals, my_rates)
    enter = lax.all_to_all(enter, ("blk", "chip"), split_axis=0, concat_axis=0, tiled=True)
    enter = enter.transpose(1, 0, 2).reshape(STATE, cols)

    attended = run_flash(flash_tables(span_order, my_blocks), q_local, kv_all)
    attention_output = lax.all_to_all(attended, ulys, split_axis=0, concat_axis=1, tiled=True)

    mine, theirs = run_correct(
        core_arr, delta, y_local, enter, params, read, gate_input, gate_other, col_block
    )
    back = lax.ppermute(theirs, "core", swap)
    mine = mine.reshape(half, chip_count, shard_cols)
    back = back.reshape(half, chip_count, shard_cols)
    even = jnp.where(core == 0, mine, back)
    odd = jnp.where(core == 0, back, mine)
    mamba_output = jnp.stack([even, odd], axis=2).reshape(half, inner)
    return (mamba_output, attention_output)


def solution(mesh):
    blk_count = mesh.shape["blk"]
    ulys_count = mesh.shape["ulys"]
    fine = Mesh(
        mesh.devices.reshape(blk_count, ulys_count // PAIR, PAIR), ("blk", "chip", "core")
    )
    rows = P(("blk", "chip", "core"), None)
    col = ("chip", "core")
    placed = (
        rows, rows, rows, rows,
        P(None, col), P(col), P(None, col), P(col), P(None, col), P(col),
        rows, rows, rows,
        P(),
    )
    return jax.shard_map(
        local, mesh=fine, in_specs=placed, out_specs=(rows, rows), check_vma=False
    )
```

time: 1650 us -> 659 us (0.40)
  local copies, waits for them, and re-layouts: 703 us -> 164 us
  other arithmetic: 470 us -> 20 us
  Pallas kernels: 0 us -> 294 us
  matrix products: 101 us -> 0.94 us
  waiting for transfers between devices: 168 us -> 88.7 us
  loops' own time: 75.2 us -> 0 us
  blocking collectives: 82.6 us -> 38.5 us
    slice x148 -> x6, local copies, waits for them, and re-layouts: 319 us -> 3.4 us  [the longest x1 0.97 us: local(): top = totals[0:1]]
    pallas_call x0 -> x4, Pallas kernels: none -> 294 us  [the longest x1 143 us: run_scan(): pl.pallas_call(scan_kernel, grid_spec=grid_spec, out_shape=[jax.ShapeDtyp...]
    reduce_sum x403 -> x6, other arithmetic: 220 us -> 2.11 us  [the longest x1 0.64 us: local(): my_pos = jnp.sum(jnp.where(chunk_ids == me, chunk_pos, 0))]
    convert_element_type x10 -> x5, other arithmetic: 107 us -> 4.52 us  [the longest x1 1.81 us: flash_tables(): first = (place == 0).astype(jnp.int32)]
    dot_general x20 -> x1, matrix products: 101 us -> 0.94 us  [local(): jnp.einsum('m,mkc->kc', before, tails, preferred_element_type=jnp.float32)]
    mul x129 -> x1, local copies, waits for them, and re-layouts: 98.7 us -> 0.04 us  [local(): -LOG2E * jnp.exp(params[:, :STATE].transpose(1, 0, 2).reshape(STATE, cols))]
    dynamic_update_slice x128 -> x0, local copies, waits for them, and re-layouts: 94.4 us -> none  [token_scan(): return lax.scan(advance, start_state, steps_in, unroll=8)]
    all_to_all x5 -> x6, waiting for transfers between devices: 166 us -> 88.6 us  [the longest x1 49 us: local(): lax.all_to_all(attended, ulys, split_axis=0, concat_axis=1, tiled=True)]
where the time goes in v1:
time: 659 us; the launch traced here: 652 us
  Pallas kernels  294 us (45%)
  local copies, waits for them, and re-layouts  164 us (25%)
  waiting for transfers between devices  88.7 us (13%)
  blocking collectives  38.5 us (6%)
  starting transfers between devices  29.3 us (4%)
  other arithmetic  20 us (3%)
  between operations  15.9 us (2%)
    pallas_call x1, Pallas kernels, run_scan(): pl.pallas_call(scan_kernel, grid_spec=grid_spec, out_shape=[jax.ShapeDtyp...  143 us
    pallas_call x1, Pallas kernels, run_correct(): pl.pallas_call(correct_kernel, grid_spec=grid_spec, out_shape=[jax.ShapeD...  87.9 us
    pallas_call x1, Pallas kernels, run_flash(): pl.pallas_call(functools.partial(flash_kernel, heads=heads, rows=rows), g...  61.3 us
    dynamic_slice x1, local copies, waits for them, and re-layouts, other_half(): picked = lax.dynamic_index_in_dim(parts, 1 - core, 2, False)  56.1 us
    all_to_all x1, waiting for transfers between devices, local(): lax.all_to_all(attended, ulys, split_axis=0, concat_axis=1, tiled=True)  49 us
    all_gather x1, blocking collectives, local(): params = lax.all_gather(packed, 'chip', axis=0, tiled=False)  34.2 us
    reshape x2, local copies, waits for them, and re-layouts, other_half(): parts = array.reshape(half, chip_count, PAIR, shard_cols)  29 us
    all_to_all x1, waiting for transfers between devices, local(): lax.all_to_all(kv_rows, ulys, split_axis=1, concat_axis=0, tiled=True)  24.3 us
  transfers between devices with their start and end apart: 11, of which 4 were waited for; matrix products, arithmetic and copies ran while one was open for 19% of the time, Pallas kernels for 45%

profile of v1, /device:TPU:0, one launch (start us, length us, event | category | flops | bytes accessed | tf_op | source)
XLA Modules:
  0.0 651.6 jit_solution(7733489823433617261)
XLA Ops:
  7.2 1.5 copy-done
  8.8 0.9 constant_dynamic-slice_fusion.1
  9.7 14.6 %reshape.177 = bf16[256,4,2,2048]{3,2,1,0:T(2,128)(2,1)} reshape(bf16[256,16384]{1,0:T(8,128)(2,1)} %own_ref.1) | data formatting | bytes 16777216 | tf_op jit(solution)/shard_map/reshape | solution.py:427
  24.2 14.4 %reshape.184 = bf16[256,4,2,2048]{3,2,1,0:T(2,128)(2,1)} reshape(bf16[256,16384]{1,0:T(8,128)(2,1)} %own_gate_ref.1) | data formatting | bytes 16777216 | tf_op jit(solution)/shard_map/reshape | solution.py:427
  38.7 56.1 %dynamic-slice_reduce_fusion = (bf16[256,4,2048]{2,1,0:T(4,128)(2,1)S(1)}, bf16[256,4,2048]{2,1,0:T(4,128)(2,1)}) fusion(bf16[256,4,2,2048]{3,2,1,0:T(2,128)(2,1)} %reshape.184, s32[]{:T(128)S(6)} %select_n.130, bf16[256,4,2,2048]{3,2,1,0:T(2,128)(2,1)} %reshape.177), kind=kLoop, calls=%fused_computation.1 | loop fusion | bytes 16777220 | tf_op jit(solution)/shard_map/jit(dynamic_index_in_dim)/dynamic_slice | solution.py:428
  94.8 8.6 %copy.60 = bf16[32,8,4,2048]{3,1,2,0:T(8,128)(2,1)} copy(bf16[32,8,4,2048]{3,2,1,0:T(4,128)(2,1)} %bitcast.62) | data formatting | bytes 8388608
  103.4 0.5 collective-permute-start
  103.9 6.7 %copy.62 = bf16[32,8,4,2048]{3,1,2,0:T(8,128)(2,1)} copy(bf16[32,8,4,2048]{3,2,1,0:T(4,128)(2,1)S(1)} %bitcast.61) | data formatting | bytes 8388608
  110.8 0.1 pad_maximum_fusion.1
  110.9 1.1 copy.49
  112.0 1.5 all_to_all.58
  113.5 6.8 %all-to-all-start.4 = ((bf16[256,8,256]{2,0,1:T(8,128)(2,1)}), bf16[256,8,256]{2,0,1:T(8,128)(2,1)S(1)}, u32[]{:S(2)}, u32[]{:S(2)}) async-start(bf16[256,8,256]{2,0,1:T(8,128)(2,1)} %all_to_all.58), calls=%async_computation.4 | async-start | bytes 2097152 | tf_op jit(solution)/shard_map/all_to_all | solution.py:404
  120.4 2.0 all_gather.26
  122.4 0.9 slice.45
  123.4 24.3 %all-to-all-done.4 = bf16[256,8,256]{2,0,1:T(8,128)(2,1)S(1)} async-done(((bf16[256,8,256]{2,0,1:T(8,128)(2,1)}), bf16[256,8,256]{2,0,1:T(8,128)(2,1)S(1)}, u32[]{:S(2)}, u32[]{:S(2)}) %all-to-all-start.4) | async-done | bytes 1048608 | tf_op jit(solution)/shard_map/all_to_all | solution.py:404
  147.7 1.4 broadcast_in_dim.128
  149.1 3.8 all-to-all-start
  153.0 0.8 copy.41.read_ref
  153.8 0.1 copy.40
  153.9 0.1 reshape.187
  154.2 0.6 fusion.10
  155.6 2.3 all_gather.21.low_ref
  158.0 34.2 %all-gather.1 = f32[96,2048]{1,0:T(8,128)} all-gather(f32[24,2048]{1,0:T(8,128)S(1)} %concatenate.10), channel_id=3, replica_groups=mesh['blk'=4,'chip'=4,'core'=2] {'chip'}, dimensions={0}, use_global_device_ids=true | all-gather | bytes 983040 | tf_op jit(solution)/shard_map/all_gather | solution.py:424
  192.2 0.9 fusion
  193.2 0.7 concatenate.9.halo_ref
  193.9 2.5 broadcast_in_dim.135.inject_ref
  196.5 142.6 %token_scan.1 = (f32[512,8192]{1,0:T(8,128)}, bf16[512,8192]{1,0:T(8,128)(2,1)}, f32[16,8192]{1,0:T(8,128)}, f32[8,8192]{1,0:T(8,128)}) custom-call(s32[1]{0:T(128)} %bitcast.core_ref, bf16[256,16384]{1,0:T(8,128)(2,1)} %own_ref.1, bf16[256,8192]{1,0:T(8,128)(2,1)} %collective-permute-done.other_ref, bf16[8,8192]{1,0:T(8,128)(2,1)} %concatenate.9.halo_ref, ...), custom_call_target="tpu_custom_call" | custom-call | tf_op jit(solution)/shard_map/token_scan/pallas_call | solution.py:249
  339.1 1.1 fusion.12
  340.2 1.0 slice.73
  341.1 1.1 convert_element_type.40
  342.2 0.1 pad_maximum_fusion.2
  342.4 0.1 copy.61
  342.5 0.9 copy.71
  343.4 5.8 all-to-all-start.1
  349.4 0.6 select_reduce_fusion.order_ref
  350.0 0.6 constant_dynamic-slice_fusion.rate_ref
  350.6 9.6 %all-to-all-done.1 = bf16[16,19,512]{2,1,0:T(8,128)(2,1)S(1)} async-done(((bf16[16,19,512]{2,1,0:T(8,128)(2,1)}), bf16[16,19,512]{2,1,0:T(8,128)(2,1)S(1)}, u32[]{:S(2)}, u32[]{:S(2)}) %all-to-all-start.1) | async-done | bytes 311328 | tf_op jit(solution)/shard_map/all_to_all | solution.py:482
  360.4 0.6 broadcast_in_dim.141.total_ref
  361.0 0.9 slice.50.end_ref
  361.9 2.7 state_combine.1
  364.5 3.5 all-to-all-start.2
  368.1 3.1 copy.70
  371.2 5.7 all-to-all-done.2
  376.9 3.6 all-to-all-start.3
  380.6 0.7 fusion.15
  381.8 0.7 copy.58
  382.5 87.9 %state_correction.1 = (bf16[256,8192]{1,0:T(8,128)(2,1)}, bf16[256,8192]{1,0:T(8,128)(2,1)}) custom-call(s32[1]{0:T(128)} %bitcast.core_ref, f32[512,8192]{1,0:T(8,128)} %get-tuple-element.8.delta_ref, bf16[512,8192]{1,0:T(8,128)(2,1)} %get-tuple-element.9.y_ref, bf16[16,8192]{1,0:T(8,128)(2,1)} %bitcast.80, f32[4,24,2048]{2,1,0:T(8,128)} %bitcast.64, ...), custom_call_target="tpu_custom_call" | custom-call | tf_op jit(solution)/shard_map/state_correction/pallas_call | solution.py:300
  470.4 0.4 collective-permute-start.2
  470.8 0.5 compare_convert_fusion.2.side_ref
  471.3 1.8 compare_convert_fusion
  473.1 0.1 select_reduce_fusion.2
  473.2 0.6 select_reduce_fusion.1.block_ref
  473.9 1.3 copy-done.3
  475.2 61.3 %causal_attention.1 = bf16[2048,512]{1,0:T(8,128)(2,1)} custom-call(s32[9]{0:T(128)} %compare_convert_fusion.2.side_ref, s32[9]{0:T(128)} %select_reduce_fusion.1.block_ref, s32[9]{0:T(128)} %get-tuple-element.27.diag_ref.last_ref, s32[9]{0:T(128)} %get-tuple-element.26.first_ref, s32[9]{0:T(128)} %get-tuple-element.27.diag_ref.last_ref, ...), custom_call_target="tpu_custom_call" | custom-call | tf_op jit(solution)/shard_map/causal_attention/pallas_call | solution.py:340
  536.4 4.8 all-to-all-start.5
  541.2 49.0 %all-to-all-done.5 = bf16[8,256,512]{2,1,0:T(8,128)(2,1)S(1)} async-done(((bf16[8,256,512]{2,1,0:T(8,128)(2,1)}), bf16[8,256,512]{2,1,0:T(8,128)(2,1)S(1)}, u32[]{:S(2)}, u32[]{:S(2)}) %all-to-all-start.5) | async-done | bytes 2097184 | tf_op jit(solution)/shard_map/all_to_all | solution.py:494
  590.2 1.6 copy.59
  591.8 1.3 copy-done.4
  593.2 5.2 broadcast_select_fusion.1
  598.4 7.8 %select_n.145 = bf16[256,4,1,2048]{3,1,0,2:T(4,128)(2,1)} reshape(bf16[256,8192]{1,0:T(8,128)(2,1)} %get-tuple-element.16) | data formatting | bytes 8388608 | tf_op jit(solution)/shard_map/jit(_where)/select_n | solution.py:502
  606.3 7.8 %select_n.147 = bf16[256,4,1,2048]{3,1,0,2:T(4,128)(2,1)} reshape(bf16[256,8192]{1,0:T(8,128)(2,1)} %get-tuple-element.17) | data formatting | bytes 8388608 | tf_op jit(solution)/shard_map/jit(_where)/select_n | solution.py:503
  614.1 7.6 %pad_maximum_fusion = bf16[256,4,2,2048]{3,1,0,2:T(4,128)(2,1)S(1)} fusion(bf16[256,4,1,2048]{3,1,0,2:T(4,128)(2,1)} %select_n.147, bf16[256,4,1,2048]{3,1,0,2:T(4,128)(2,1)} %select_n.145), kind=kLoop, calls=%fused_computation | loop fusion | flops 4194304 | bytes 16777216 | tf_op jit(solution)/shard_map/stack | solution.py:504
  621.7 8.3 %copy.47 = bf16[256,4,2,2048]{3,2,1,0:T(2,128)(2,1)} copy(bf16[256,4,2,2048]{3,1,0,2:T(4,128)(2,1)S(1)} %pad_maximum_fusion) | data formatting | bytes 16777216 | tf_op jit(solution)/shard_map/stack | solution.py:504
  630.0 14.6 %reshape.186 = bf16[256,16384]{1,0:T(8,128)(2,1)} reshape(bf16[256,4,2,2048]{3,2,1,0:T(2,128)(2,1)} %copy.47) | data formatting | bytes 16777216 | tf_op jit(solution)/shard_map/reshape | solution.py:504
  (63 shorter events, 1.2 us)
Async XLA Ops:
  7.2 1.6 copy-start
  7.2 186.8 %all-gather.7.cloned.1.call-start = ((), (), s32[]{:S(2)}) async-start(), calls=%async_computation.7 | async-start | bytes 8912896 | tf_op jit(solution)/shard_map/all_gather | solution.py:411
  103.4 19.0 %collective-permute-start = (bf16[256,8192]{1,0:T(8,128)(2,1)}, bf16[256,8192]{1,0:T(8,128)(2,1)}, u32[]{:S(2)}, u32[]{:S(2)}) collective-permute-start(bf16[256,8192]{1,0:T(8,128)(2,1)} %bitcast.35), channel_id=1, source_target_pairs={{0,1},{1,0},{2,3},{3,2},{4,5},{5,4},{6,7},{7,6},{8,9},{9,8},{10,11... | collective-permute-start | bytes 12582920 | tf_op jit(solution)/shard_map/ppermute | solution.py:431
  103.9 6.7 %copy-start.6 = (bf16[256,1024]{1,0:T(8,128)(2,1)S(1)}, bf16[256,1024]{1,0:T(8,128)(2,1)}, u32[]{:S(2)}) copy-start(bf16[256,1024]{1,0:T(8,128)(2,1)} %param.25) | copy-start | bytes 1572868
  103.9 6.8 %copy-start.7 = (bf16[256,1024]{1,0:T(8,128)(2,1)S(1)}, bf16[256,1024]{1,0:T(8,128)(2,1)}, u32[]{:S(2)}) copy-start(bf16[256,1024]{1,0:T(8,128)(2,1)} %param.26) | copy-start | bytes 1572868
  110.6 272.0 %collective-permute-start.1 = (bf16[256,8192]{1,0:T(8,128)(2,1)}, bf16[256,8192]{1,0:T(8,128)(2,1)}, u32[]{:S(2)}, u32[]{:S(2)}) collective-permute-start(bf16[256,8192]{1,0:T(8,128)(2,1)} %bitcast.40), channel_id=1, source_target_pairs={{0,1},{1,0},{2,3},{3,2},{4,5},{5,4},{6,7},{7,6},{8,9},{9,8},{10,11... | collective-permute-start | bytes 12582920 | tf_op jit(solution)/shard_map/ppermute | solution.py:432
  110.8 9.6 %slice-start = ((bf16[256,16384]{1,0:T(8,128)(2,1)}), bf16[8,16384]{1,0:T(8,128)(2,1)S(1)}, s32[]{:S(2)}) async-start(bf16[256,16384]{1,0:T(8,128)(2,1)} %own_ref.1), calls=%async_computation.8 | async-start | bytes 524288 | tf_op jit(solution)/shard_map/slice | solution.py:457
  110.8 9.6 %copy-start.10 = (bf16[256,32]{0,1:T(8,128)(2,1)S(1)}, bf16[256,32]{0,1:T(8,128)(2,1)}, u32[]{:S(2)}) copy-start(bf16[256,32]{0,1:T(8,128)(2,1)} %param.17) | copy-start | bytes 49156
  113.5 40.6 %copy-start.15 = (s32[8]{0:T(128)S(1)}, s32[8]{0:T(128)}, u32[]{:S(2)}) copy-start(s32[8]{0:T(128)} %param.27) | copy-start | bytes 100
  113.5 42.0 %copy-start.9 = (f32[16,2048]{1,0:T(8,128)S(1)}, f32[16,2048]{1,0:T(8,128)}, u32[]{:S(2)}) copy-start(f32[16,2048]{1,0:T(8,128)} %param.22) | copy-start | bytes 393220
  113.5 42.0 %copy-start.11 = (bf16[4,2048]{1,0:T(4,128)(2,1)S(1)}, bf16[4,2048]{1,0:T(4,128)(2,1)}, u32[]{:S(2)}) copy-start(bf16[4,2048]{1,0:T(4,128)(2,1)} %param.18) | copy-start | bytes 49156
  113.5 42.0 %copy-start.12 = (f32[2048]{0:T(1024)S(1)}, f32[2048]{0:T(1024)}, u32[]{:S(2)}) copy-start(f32[2048]{0:T(1024)} %param.19) | copy-start | bytes 24580
  113.5 42.0 %copy-start.13 = (f32[2048]{0:T(1024)S(1)}, f32[2048]{0:T(1024)}, u32[]{:S(2)}) copy-start(f32[2048]{0:T(1024)} %param.21) | copy-start | bytes 24580
  113.5 42.0 %copy-start.14 = (f32[2048]{0:T(1024)S(1)}, f32[2048]{0:T(1024)}, u32[]{:S(2)}) copy-start(f32[2048]{0:T(1024)} %param.23) | copy-start | bytes 24580
  113.5 42.1 %copy-start.8 = (bf16[256,512]{1,0:T(8,128)(2,1)S(1)}, bf16[256,512]{1,0:T(8,128)(2,1)}, u32[]{:S(2)}) copy-start(bf16[256,512]{1,0:T(8,128)(2,1)} %param.16) | copy-start | bytes 786436
  113.5 34.1 %all-to-all-start.4 = ((bf16[256,8,256]{2,0,1:T(8,128)(2,1)}), bf16[256,8,256]{2,0,1:T(8,128)(2,1)S(1)}, u32[]{:S(2)}, u32[]{:S(2)}) async-start(bf16[256,8,256]{2,0,1:T(8,128)(2,1)} %all_to_all.58), calls=%async_computation.4 | async-start | bytes 2097152 | tf_op jit(solution)/shard_map/all_to_all | solution.py:404
  147.7 44.5 %copy-start.5 = (bf16[256,8,256]{2,0,1:T(8,128)(2,1)}, bf16[256,8,256]{2,0,1:T(8,128)(2,1)S(1)}, u32[]{:S(2)}) copy-start(bf16[256,8,256]{2,0,1:T(8,128)(2,1)S(1)} %all-to-all-done.4) | copy-start | bytes 3145732
  149.1 43.2 %all-to-all-start = ((bf16[16,3,8192]{2,1,0:T(4,128)(2,1)}), bf16[16,3,8192]{2,1,0:T(4,128)(2,1)S(1)}, u32[]{:S(2)}, u32[]{:S(2)}) async-start(bf16[16,3,8192]{2,1,0:T(4,128)(2,1)} %broadcast_in_dim.128), calls=%async_computation | async-start | bytes 2097152 | tf_op jit(solution)/shard_map/all_to_all | solution.py:460
  152.8 321.0 %all-gather.5.cloned.1.call-start = ((), (), s32[]{:S(2)}) async-start(), calls=%async_computation.6 | async-start | bytes 5242880 | tf_op jit(solution)/shard_map/all_gather | solution.py:405
  339.1 10.2 %copy-start.2 = (f32[96,2048]{1,0:T(8,128)S(1)}, f32[96,2048]{1,0:T(8,128)}, u32[]{:S(2)}) copy-start(f32[96,2048]{1,0:T(8,128)} %all-gather.1) | copy-start | bytes 2359300
  343.4 16.8 %all-to-all-start.1 = ((bf16[16,19,512]{2,1,0:T(8,128)(2,1)}), bf16[16,19,512]{2,1,0:T(8,128)(2,1)S(1)}, u32[]{:S(2)}, u32[]{:S(2)}) async-start(bf16[16,19,512]{2,1,0:T(8,128)(2,1)} %bitcast.58), calls=%async_computation.1 | async-start | bytes 786432 | tf_op jit(solution)/shard_map/all_to_all | solution.py:482
  364.5 12.3 %all-to-all-start.2 = ((bf16[16,16,512]{2,1,0:T(8,128)(2,1)}), bf16[16,16,512]{2,1,0:T(8,128)(2,1)S(1)}, u32[]{:S(2)}, u32[]{:S(2)}) async-start(bf16[16,16,512]{2,1,0:T(8,128)(2,1)} %state_combine.1), calls=%async_computation.2 | async-start | bytes 524288 | tf_op jit(solution)/shard_map/all_to_all | solution.py:490
  376.9 97.0 %all-to-all-start.3 = ((bf16[256,8,512]{2,0,1:T(8,128)(2,1)}), bf16[256,8,512]{2,0,1:T(8,128)(2,1)S(1)}, u32[]{:S(2)}, u32[]{:S(2)}) async-start(bf16[256,8,512]{2,0,1:T(8,128)(2,1)} %bitcast.69), calls=%async_computation.3 | async-start | bytes 4194304 | tf_op jit(solution)/shard_map/all_to_all | solution.py:406
  470.4 121.4 %collective-permute-start.2 = (bf16[256,8192]{1,0:T(8,128)(2,1)}, bf16[256,8192]{1,0:T(8,128)(2,1)}, u32[]{:S(2)}, u32[]{:S(2)}) collective-permute-start(bf16[256,8192]{1,0:T(8,128)(2,1)} %get-tuple-element.13), channel_id=1, source_target_pairs={{0,1},{1,0},{2,3},{3,2},{4,5},{5,4},{6,7},{7,6},{8,9},{9,8},{10,11... | collective-permute-start | bytes 12582920 | tf_op jit(solution)/shard_map/ppermute | solution.py:499
  473.8 1.3 copy-start.3
  536.4 53.8 %all-to-all-start.5 = ((bf16[8,256,512]{2,1,0:T(8,128)(2,1)}), bf16[8,256,512]{2,1,0:T(8,128)(2,1)S(1)}, u32[]{:S(2)}, u32[]{:S(2)}) async-start(bf16[8,256,512]{2,1,0:T(8,128)(2,1)} %bitcast.67), calls=%async_computation.5 | async-start | bytes 4194304 | tf_op jit(solution)/shard_map/all_to_all | solution.py:494
  590.2 2.9 copy-start.4
  630.0 14.6 %copy-start.1 = (bf16[512,2048]{1,0:T(8,128)(2,1)S(1)}, bf16[512,2048]{1,0:T(8,128)(2,1)}, u32[]{:S(2)}) copy-start(bf16[512,2048]{1,0:T(8,128)(2,1)} %param.20) | copy-start | bytes 6291460
Sparse Core Ops, SparseCore 0:
  10.8 115.8 all-gather.6
  192.3 52.9 all-gather.4

commit v2 on v1

v2 whole, which is shorter than its diff:
```python
import functools

import jax
import jax.numpy as jnp
from jax import lax
from jax.experimental import pallas as pl
from jax.experimental.pallas import tpu as pltpu
from jax.sharding import Mesh
from jax.sharding import PartitionSpec as P

STATE = 16
CONV = 4
HD = 128
SPAN = 1024
LANES = 128
PAIR = 2
GROUP = 16
PIECES = 2
NEG_LARGE = -1e30
LOG2E = 1.4426950408889634
PARAM_ROWS = 24
VMEM_LIMIT = 56 * 1024 * 1024


def softplus(x):
    return jnp.maximum(x, 0.0) + jnp.log1p(jnp.exp(-jnp.abs(x)))


def silu(x):
    half = 0.5 * x
    return half * jnp.tanh(half) + half


def lane_tiles(cols):
    size = min(LANES, cols)
    return [slice(at, at + size) for at in range(0, cols, size)]


def spread(ref, k, row, count):
    return jnp.broadcast_to(ref[k, pl.ds(row, 1), :], (count, ref.shape[2]))


def scan_kernel(
    core_ref, own_ref, other_ref, halo_ref, low_own_ref, low_other_ref, weight_ref, param_ref,
    inject_ref, read_ref,
    delta_ref, y_ref, sent_ref,
    x_scr, driven_scr, push_scr, hist_scr, rate_scr, param_scr,
):
    core = core_ref[0]
    tokens, cols = y_ref.shape
    half = tokens // 2
    depth = low_own_ref.shape[1]
    tiles = lane_tiles(cols)
    mine = pl.multiple_of(core * half, 8)
    theirs = pl.multiple_of((1 - core) * half, 8)
    weight = weight_ref[...].reshape(depth, cols)
    raw_mine = jnp.dot(low_own_ref[...], weight, preferred_element_type=jnp.float32)
    for k, tile in enumerate(tiles):
        delta_ref[k, pl.ds(mine, half), :] = raw_mine[:, tile]
    raw_theirs = jnp.dot(low_other_ref[...], weight, preferred_element_type=jnp.float32)
    for k, tile in enumerate(tiles):
        delta_ref[k, pl.ds(theirs, half), :] = raw_theirs[:, tile]
    for k, tile in enumerate(tiles):
        x_scr[k, 0:8, :] = halo_ref[:, tile].astype(jnp.float32)
        x_scr[k, pl.ds(8 + mine, half), :] = own_ref[:, tile].astype(jnp.float32)
        x_scr[k, pl.ds(8 + theirs, half), :] = other_ref[:, tile].astype(jnp.float32)
    rate_scr[...] = -LOG2E * jnp.exp(param_ref[0, :STATE, :])
    for k in range(CONV + 3):
        param_scr[8 * k : 8 * k + 8, :] = jnp.broadcast_to(
            param_ref[0, STATE + k : STATE + k + 1, :], (8, cols)
        )

    def prepare(step, total):
        first = pl.multiple_of(step * 8, 8)
        total = list(total)
        for k, tile in enumerate(tiles):
            mixed = param_scr[8 * CONV : 8 * CONV + 8, tile]
            for j in range(CONV):
                shifted = x_scr[k, pl.ds(first + 8 - (CONV - 1) + j, 8), :]
                mixed = mixed + param_scr[8 * j : 8 * j + 8, tile] * shifted
            driven = silu(mixed)
            delta = softplus(
                delta_ref[k, pl.ds(first, 8), :] + param_scr[8 * CONV + 8 : 8 * CONV + 16, tile]
            )
            delta_ref[k, pl.ds(first, 8), :] = delta
            driven_scr[pl.ds(first, 8), tile] = driven * param_scr[8 * CONV + 16 : 8 * CONV + 24, tile]
            push_scr[k, pl.ds(first, 8), :] = driven * delta
            total[k] = total[k] + delta
        return tuple(total)

    zero = jnp.zeros((8, tiles[0].stop), jnp.float32)
    total = lax.fori_loop(0, tokens // 8, prepare, (zero,) * len(tiles))
    total = jnp.sum(jnp.concatenate(total, axis=1), axis=0, keepdims=True)

    def step16(group, hidden):
        base = pl.multiple_of(group * GROUP, GROUP)
        hidden = list(hidden)
        for i in range(GROUP):
            inject = inject_ref[pl.ds(pl.multiple_of((base + i) * STATE, STATE), STATE), :]
            for k, tile in enumerate(tiles):
                decay = jnp.exp2(spread(delta_ref, k, base + i, STATE) * rate_scr[:, tile])
                push = spread(push_scr, k, base + i, STATE)
                hidden[k] = decay * hidden[k] + push * inject
            hist_scr[i * STATE : (i + 1) * STATE, :] = jnp.concatenate(hidden, axis=1).astype(
                jnp.bfloat16
            )
        read = read_ref[pl.ds(base, GROUP), :]
        out = jnp.dot(read, hist_scr[...], preferred_element_type=jnp.float32)
        y_ref[pl.ds(base, GROUP), :] = (out + driven_scr[pl.ds(base, GROUP), :]).astype(y_ref.dtype)
        return tuple(hidden)

    zero = jnp.zeros((STATE, tiles[0].stop), jnp.float32)
    end = lax.fori_loop(0, tokens // GROUP, step16, (zero,) * len(tiles))
    end = jnp.concatenate(end, axis=1)
    top = total.astype(jnp.bfloat16).astype(jnp.float32)
    mid = (total - top).astype(jnp.bfloat16).astype(jnp.float32)
    low = total - top - mid
    row = lax.broadcasted_iota(jnp.int32, (STATE, cols), 0)
    rows = jnp.where(row == 0, top, jnp.where(row == 1, mid, jnp.where(row == 2, low, 0.0)))
    sent_ref[:STATE, :] = end.astype(sent_ref.dtype)
    sent_ref[STATE:, :] = rows.astype(sent_ref.dtype)


def correct_body(
    core_ref, delta_ref, y_ref, enter_ref, param_ref, read_ref, own_gate_ref, other_gate_ref,
    mine_ref, theirs_ref, hist_scr, out_scr, rate_scr,
):
    core = core_ref[0]
    tokens, cols = y_ref.shape
    half = tokens // 2
    rate_scr[...] = -LOG2E * jnp.exp(param_ref[0, :STATE, :])

    tiles = lane_tiles(cols)

    def step16(group, elapsed):
        base = pl.multiple_of(group * GROUP, GROUP)
        elapsed = list(elapsed)
        for i in range(GROUP):
            carried = []
            for k, tile in enumerate(tiles):
                elapsed[k] = elapsed[k] + spread(delta_ref, k, base + i, 8)
                twice = jnp.concatenate([elapsed[k], elapsed[k]], axis=0)
                carried.append(jnp.exp2(twice * rate_scr[:, tile]))
            carried = jnp.concatenate(carried, axis=1).astype(jnp.bfloat16)
            hist_scr[i * STATE : (i + 1) * STATE, :] = carried * enter_ref[...]
        read = read_ref[pl.ds(base, GROUP), :]
        out = jnp.dot(read, hist_scr[...], preferred_element_type=jnp.float32)
        total = out + y_ref[pl.ds(base, GROUP), :].astype(jnp.float32)
        out_scr[pl.ds(base, GROUP), :] = total.astype(jnp.bfloat16).astype(jnp.float32)
        return tuple(elapsed)

    zero = jnp.zeros((8, tiles[0].stop), jnp.float32)
    lax.fori_loop(0, tokens // GROUP, step16, (zero,) * len(tiles))
    rows = 16

    def gated(gate_ref, dest_ref, offset):
        def body(step, carry):
            first = pl.multiple_of(step * rows, rows)
            gate = gate_ref[pl.ds(first, rows), :].astype(jnp.float32)
            value = out_scr[pl.ds(pl.multiple_of(offset + first, 8), rows), :]
            dest_ref[pl.ds(first, rows), :] = (value * silu(gate)).astype(dest_ref.dtype)
            return carry

        lax.fori_loop(0, half // rows, body, 0)

    gated(own_gate_ref, mine_ref, core * half)
    gated(other_gate_ref, theirs_ref, (1 - core) * half)


def correct_kernel(core_ref, *refs, resumed):
    correct_body(core_ref, *(refs[1:] if resumed else refs))


def combine_kernel(order_ref, got_ref, rate_ref, enter_ref):
    chunks = got_ref.shape[0]
    rates = rate_ref[...]

    def body(place, state):
        chunk = order_ref[place]
        enter_ref[chunk] = state.astype(enter_ref.dtype)
        got = got_ref[chunk].astype(jnp.float32)
        total = got[STATE : STATE + 1] + got[STATE + 1 : STATE + 2] + got[STATE + 2 : STATE + 3]
        return jnp.exp2(total * rates) * state + got[:STATE]

    lax.fori_loop(0, chunks, body, jnp.zeros(rates.shape, jnp.float32))


def copy_kernel(core_ref, in_ref, out_ref):
    out_ref[...] = in_ref[...]


def place_kernel(core_ref, buffer_ref, in_ref, out_ref):
    out_ref[...] = in_ref[...]


def flash_kernel(
    side_ref, block_ref, diag_ref, first_ref, last_ref, q_ref, kv_ref, out_ref,
    max_scr, acc_scr, value_scr, *, heads, rows,
):
    step = pl.program_id(0)
    scale = LOG2E * HD ** (-0.5)
    span = kv_ref.shape[0]
    value_scr[:, :HD] = kv_ref[:, HD:]
    value_scr[:, HD:] = jnp.ones((span, HD), jnp.bfloat16)

    @pl.when(first_ref[step] == 1)
    def _():
        max_scr[...] = jnp.full(max_scr.shape, NEG_LARGE, jnp.float32)
        acc_scr[...] = jnp.zeros(acc_scr.shape, jnp.float32)

    def absorb(head, row, key_count, masked):
        q = q_ref[row : row + rows, head * HD : (head + 1) * HD]
        scores = lax.dot_general(
            q, kv_ref[:key_count, :HD], (((1,), (1,)), ((), ())),
            preferred_element_type=jnp.float32,
        ) * scale
        if masked:
            query_at = lax.broadcasted_iota(jnp.int32, scores.shape, 0) + row
            key_at = lax.broadcasted_iota(jnp.int32, scores.shape, 1)
            scores = jnp.where(key_at <= query_at, scores, NEG_LARGE)
        at = slice(head * span + row, head * span + row + rows)
        old_max = max_scr[at, :]
        new_max = jnp.maximum(old_max, jnp.max(scores, axis=1, keepdims=True))
        weights = jnp.exp2(scores - new_max[:, :1]).astype(jnp.bfloat16)
        shrink = jnp.exp2(old_max - new_max)
        acc_scr[at, :] = acc_scr[at, :] * shrink[:, :1] + jnp.dot(
            weights, value_scr[:key_count, :], preferred_element_type=jnp.float32
        )
        max_scr[at, :] = new_max

    @pl.when(diag_ref[step] == 0)
    def _():
        for head in range(heads):
            for row in range(0, span, rows):
                absorb(head, row, span, False)

    @pl.when(diag_ref[step] == 1)
    def _():
        for head in range(heads):
            for row in range(0, span, rows):
                absorb(head, row, row + rows, True)

    @pl.when(last_ref[step] == 1)
    def _():
        for head in range(heads):
            for row in range(0, span, rows):
                at = slice(head * span + row, head * span + row + rows)
                out_ref[row : row + rows, head * HD : (head + 1) * HD] = (
                    acc_scr[at, :HD] / acc_scr[at, HD:]
                ).astype(out_ref.dtype)


def whole(shape):
    return pl.BlockSpec(
        shape, lambda j, core_ref: (0,) * len(shape), pipeline_mode=pl.Buffered(1)
    )


def shard_map_of(side, piece):
    return lambda j, core_ref: (0, (PAIR * j + (core_ref[0] + side) % PAIR) * PIECES + piece)


def plain(j, core_ref):
    return (0, j)


def run_pick(core, full, piece, width):
    half, inner = full.shape
    blocks = inner // (width * PIECES * PAIR)
    return pl.pallas_call(
        copy_kernel,
        grid_spec=pltpu.PrefetchScalarGridSpec(
            num_scalar_prefetch=1,
            grid=(blocks,),
            in_specs=[pl.BlockSpec((half, width), shard_map_of(1, piece))],
            out_specs=pl.BlockSpec((half, width), plain),
        ),
        out_shape=jax.ShapeDtypeStruct((half, blocks * width), full.dtype),
        name="pick_channels",
    )(core, full)


def run_place(core, full, part, piece, width):
    half, _ = full.shape
    blocks = part.shape[1] // width
    return pl.pallas_call(
        place_kernel,
        grid_spec=pltpu.PrefetchScalarGridSpec(
            num_scalar_prefetch=1,
            grid=(blocks,),
            in_specs=[pl.BlockSpec(memory_space=pl.ANY), pl.BlockSpec((half, width), plain)],
            out_specs=pl.BlockSpec((half, width), shard_map_of(1, piece)),
        ),
        out_shape=jax.ShapeDtypeStruct(full.shape, full.dtype),
        input_output_aliases={1: 0},
        name="place_channels",
    )(core, full, part)


def run_scan(core, x_own, x_other, halo, low_own, low_other, weight, params, inject, read, piece):
    half, cols = x_other.shape
    tokens = 2 * half
    parts, blocks, part_rows, width = weight.shape
    lanes = min(LANES, width)
    tiles = width // lanes
    return pl.pallas_call(
        scan_kernel,
        grid_spec=pltpu.PrefetchScalarGridSpec(
            num_scalar_prefetch=1,
            grid=(blocks,),
            in_specs=[
                pl.BlockSpec((half, width), shard_map_of(0, piece)),
                pl.BlockSpec((half, width), plain),
                pl.BlockSpec((8, width), plain),
                whole(low_own.shape),
                whole(low_other.shape),
                pl.BlockSpec((parts, 1, part_rows, width), lambda j, core_ref: (0, j, 0, 0)),
                pl.BlockSpec((1, PARAM_ROWS, width), lambda j, core_ref: (j, 0, piece)),
                whole(inject.shape),
                whole(read.shape),
            ],
            out_specs=[
                pl.BlockSpec((tiles, tokens, lanes), lambda j, core_ref: (j, 0, 0)),
                pl.BlockSpec((tokens, width), plain),
                pl.BlockSpec((2 * STATE, width), plain),
            ],
            scratch_shapes=[
                pltpu.VMEM((tiles, tokens + 8, lanes), jnp.float32),
                pltpu.VMEM((tokens, width), jnp.float32),
                pltpu.VMEM((tiles, tokens, lanes), jnp.float32),
                pltpu.VMEM((GROUP * STATE, width), jnp.bfloat16),
                pltpu.VMEM((STATE, width), jnp.float32),
                pltpu.VMEM((8 * (CONV + 3), width), jnp.float32),
            ],
        ),
        out_shape=[
            jax.ShapeDtypeStruct((cols // lanes, tokens, lanes), jnp.float32),
            jax.ShapeDtypeStruct((tokens, cols), jnp.bfloat16),
            jax.ShapeDtypeStruct((2 * STATE, cols), jnp.bfloat16),
        ],
        compiler_params=pltpu.CompilerParams(vmem_limit_bytes=VMEM_LIMIT),
        name="token_scan",
    )(core, x_own, x_other, halo, low_own, low_other, weight, params, inject, read)


def run_correct(core, full, delta, y, enter, params, read, gate_own, gate_other, piece, width):
    tokens, cols = y.shape
    half, inner = gate_own.shape
    blocks = cols // width
    lanes = delta.shape[2]
    tiles = width // lanes
    resumed = full is not None
    first_spec = [pl.BlockSpec(memory_space=pl.ANY)] if resumed else []
    first_arg = (full,) if resumed else ()
    return pl.pallas_call(
        functools.partial(correct_kernel, resumed=resumed),
        grid_spec=pltpu.PrefetchScalarGridSpec(
            num_scalar_prefetch=1,
            grid=(blocks,),
            in_specs=first_spec
            + [
                pl.BlockSpec((tiles, tokens, lanes), lambda j, core_ref: (j, 0, 0)),
                pl.BlockSpec((tokens, width), plain),
                pl.BlockSpec((STATE, width), plain),
                pl.BlockSpec((1, PARAM_ROWS, width), lambda j, core_ref: (j, 0, piece)),
                whole(read.shape),
                pl.BlockSpec((half, width), shard_map_of(0, piece)),
                pl.BlockSpec((half, width), plain),
            ],
            out_specs=[
                pl.BlockSpec((half, width), shard_map_of(0, piece)),
                pl.BlockSpec((half, width), plain),
            ],
            scratch_shapes=[
                pltpu.VMEM((GROUP * STATE, width), jnp.bfloat16),
                pltpu.VMEM((tokens, width), jnp.float32),
                pltpu.VMEM((STATE, width), jnp.float32),
            ],
        ),
        out_shape=[
            jax.ShapeDtypeStruct((half, inner), jnp.bfloat16),
            jax.ShapeDtypeStruct((half, cols), jnp.bfloat16),
        ],
        input_output_aliases={1: 0} if resumed else {},
        compiler_params=pltpu.CompilerParams(vmem_limit_bytes=VMEM_LIMIT),
        name="state_correction",
    )(core, *first_arg, delta, y, enter, params, read, gate_own, gate_other)


def run_combine(order, got, rates):
    chunks, _, cols = got.shape
    return pl.pallas_call(
        combine_kernel,
        grid_spec=pltpu.PrefetchScalarGridSpec(
            num_scalar_prefetch=1,
            grid=(1,),
            in_specs=[
                pl.BlockSpec(got.shape, lambda i, o: (0, 0, 0)),
                pl.BlockSpec(rates.shape, lambda i, o: (0, 0)),
            ],
            out_specs=pl.BlockSpec((chunks, STATE, cols), lambda i, o: (0, 0, 0)),
        ),
        out_shape=jax.ShapeDtypeStruct((chunks, STATE, cols), jnp.bfloat16),
        compiler_params=pltpu.CompilerParams(vmem_limit_bytes=VMEM_LIMIT),
        name="state_combine",
    )(order, got, rates)


def run_flash(tables, q, kv, rows=512):
    tokens, width = q.shape
    heads = width // HD
    steps = tables[0].shape[0]

    def q_map(s, side, block, diag, first, last):
        return (side[s], 0)

    def kv_map(s, side, block, diag, first, last):
        return (block[s], 0)

    return pl.pallas_call(
        functools.partial(flash_kernel, heads=heads, rows=rows),
        grid_spec=pltpu.PrefetchScalarGridSpec(
            num_scalar_prefetch=5,
            grid=(steps,),
            in_specs=[pl.BlockSpec((SPAN, width), q_map), pl.BlockSpec((SPAN, 2 * HD), kv_map)],
            out_specs=pl.BlockSpec((SPAN, width), q_map),
            scratch_shapes=[
                pltpu.VMEM((heads * SPAN, HD), jnp.float32),
                pltpu.VMEM((heads * SPAN, 2 * HD), jnp.float32),
                pltpu.VMEM((SPAN, 2 * HD), jnp.bfloat16),
            ],
        ),
        out_shape=jax.ShapeDtypeStruct(q.shape, jnp.bfloat16),
        compiler_params=pltpu.CompilerParams(vmem_limit_bytes=VMEM_LIMIT),
        name="causal_attention",
    )(*tables, q, kv)


def flash_tables(span_order, my_blocks):
    block_total = span_order.shape[0]
    places = jnp.arange(block_total, dtype=jnp.int32)
    holder = jnp.sum(jnp.where(span_order[None, :] == places[:, None], places[None, :], 0), axis=1)
    steps = jnp.arange(block_total + 1, dtype=jnp.int32)
    first_count = my_blocks[0] + 1
    side = (steps >= first_count).astype(jnp.int32)
    place = jnp.where(side == 1, steps - first_count, steps)
    limit = jnp.where(side == 1, my_blocks[1], my_blocks[0])
    block = jnp.sum(jnp.where(places[None, :] == place[:, None], holder[None, :], 0), axis=1)
    last = (place == limit).astype(jnp.int32)
    first = (place == 0).astype(jnp.int32)
    return (side, block.astype(jnp.int32), last, first, last)


def local(
    mamba_input, gate_input, delta_low, state_mixers, conv_weight, conv_bias, delta_weight,
    delta_bias, decay_log, skip_gain, queries, key_rows, value_rows, span_order,
):
    blk = lax.axis_index("blk")
    chip = lax.axis_index("chip")
    core = lax.axis_index("core")
    blk_count = lax.axis_size("blk")
    chip_count = lax.axis_size("chip")
    ulys = ("chip", "core")
    chips = ("blk", "chip")
    ulys_count = chip_count * PAIR
    chunks = blk_count * chip_count
    block_total = span_order.shape[0]
    half, inner = mamba_input.shape
    tokens = PAIR * half
    shard_cols = delta_weight.shape[1]
    width = shard_cols // PIECES
    cols = chip_count * width
    swap = [(0, 1), (1, 0)]
    core_arr = core.astype(jnp.int32).reshape(1)
    my_blocks = lax.dynamic_slice_in_dim(span_order, 2 * blk, 2, 0)

    depth = delta_weight.shape[0]
    part_rows = depth // blk_count
    part = lax.dynamic_slice_in_dim(delta_weight, blk * part_rows, part_rows, 0)
    weights = []
    for piece in range(PIECES):
        gathered = lax.all_gather(
            part[:, piece * width : (piece + 1) * width], chips, axis=0, tiled=False
        )
        weights.append(gathered.reshape(blk_count, chip_count, part_rows, width))
    packed = jnp.concatenate(
        [
            decay_log,
            conv_weight.astype(jnp.float32),
            conv_bias[None],
            delta_bias[None],
            skip_gain[None],
            jnp.zeros((1, shard_cols), jnp.float32),
        ],
        axis=0,
    )
    params = lax.all_to_all(
        jnp.broadcast_to(packed[None], (chip_count, PARAM_ROWS, shard_cols)), "chip",
        split_axis=0, concat_axis=0, tiled=True,
    )
    rates = -LOG2E * jnp.exp(params[:, :STATE])

    x_other = [
        lax.ppermute(run_pick(core_arr, mamba_input, piece, width), "core", swap)
        for piece in range(PIECES)
    ]
    low_other = lax.ppermute(delta_low, "core", swap)
    mixers_other = lax.ppermute(state_mixers, "core", swap)
    mixers = jnp.where(
        core == 0,
        jnp.concatenate([state_mixers, mixers_other], axis=0),
        jnp.concatenate([mixers_other, state_mixers], axis=0),
    )
    inject = jnp.broadcast_to(
        mixers[:, :STATE].astype(jnp.float32).reshape(tokens * STATE, 1), (tokens * STATE, LANES)
    )
    same = jnp.arange(tokens, dtype=jnp.int32)[:, None] % GROUP == jnp.arange(GROUP, dtype=jnp.int32)
    read = jnp.where(
        same[:, :, None], mixers[:, None, STATE:], jnp.zeros((), jnp.bfloat16)
    ).reshape(tokens, GROUP * STATE)

    per_block = SPAN // tokens
    chunk_ids = jnp.arange(chunks, dtype=jnp.int32)
    stored = chunk_ids // per_block
    block_ids = jnp.arange(block_total, dtype=jnp.int32)
    block_pos = jnp.sum(
        jnp.where(stored[:, None] == block_ids[None, :], span_order[None, :], 0), axis=1
    )
    chunk_pos = block_pos * per_block + chunk_ids % per_block
    order = jnp.sum(
        jnp.where(chunk_pos[None, :] == chunk_ids[:, None], chunk_ids[None, :], 0), axis=1
    ).astype(jnp.int32)
    me = blk * chip_count + chip
    my_pos = jnp.sum(jnp.where(chunk_ids == me, chunk_pos, 0))
    own_tail = lax.dynamic_index_in_dim(
        mamba_input[half - (CONV - 1) :].reshape(CONV - 1, chip_count, PAIR, PIECES, width),
        core, 2, False,
    )
    other_tail = jnp.stack(
        [x[half - (CONV - 1) :].reshape(CONV - 1, chip_count, width) for x in x_other], axis=2
    )
    tail = jnp.where(core == 1, own_tail, other_tail).reshape(CONV - 1, PIECES * cols)
    tails = lax.all_to_all(
        jnp.broadcast_to(tail[None], (chunks, CONV - 1, PIECES * cols)), chips,
        split_axis=0, concat_axis=0, tiled=True,
    )
    before = (chunk_pos == my_pos - 1).astype(jnp.bfloat16)
    halo = jnp.einsum("m,mkc->kc", before, tails, preferred_element_type=jnp.float32)
    halo = jnp.concatenate(
        [jnp.zeros((8 - (CONV - 1), PIECES * cols), jnp.bfloat16), halo.astype(jnp.bfloat16)],
        axis=0,
    ).reshape(8, chip_count, PIECES, width)

    kv_heads = key_rows.shape[1] // HD
    repeat = ulys_count // kv_heads
    kv_rows = jnp.stack(
        [key_rows.reshape(half, kv_heads, HD), value_rows.reshape(half, kv_heads, HD)], axis=2
    )
    kv_rows = jnp.broadcast_to(
        kv_rows[:, :, None], (half, kv_heads, repeat, 2, HD)
    ).reshape(half, ulys_count * 2 * HD)
    kv_local = lax.all_to_all(kv_rows, ulys, split_axis=1, concat_axis=0, tiled=True)
    kv_all = gather_blocks(kv_local, blk, blk_count)
    q_local = lax.all_to_all(queries, ulys, split_axis=1, concat_axis=0, tiled=True)

    def scan_piece(piece, x_piece):
        return run_scan(
            core_arr, mamba_input, x_piece, halo[:, :, piece].reshape(8, cols), delta_low,
            low_other, weights[piece], params, inject, read, piece,
        )

    share = cols // chunks

    def exchange(sent, piece):
        got = lax.all_to_all(
            sent.reshape(2 * STATE, chunks, share).transpose(1, 0, 2), chips,
            split_axis=0, concat_axis=0, tiled=True,
        )
        piece_rates = rates[:, :, piece * width : (piece + 1) * width]
        piece_rates = piece_rates.transpose(1, 0, 2).reshape(STATE, cols)
        my_rates = lax.dynamic_slice_in_dim(piece_rates, me * share, share, 1)
        enter = run_combine(order, got, my_rates)
        enter = lax.all_to_all(enter, chips, split_axis=0, concat_axis=0, tiled=True)
        return enter.transpose(1, 0, 2).reshape(STATE, cols)

    delta_0, y_0, sent_0 = scan_piece(0, x_other[0])
    q_local, sent_0 = lax.optimization_barrier((q_local, sent_0))
    attended = run_flash(flash_tables(span_order, my_blocks), q_local, kv_all)
    x_later, attended = lax.optimization_barrier((x_other[1], attended))
    attention_output = lax.all_to_all(attended, ulys, split_axis=0, concat_axis=1, tiled=True)
    enter_0 = exchange(sent_0, 0)
    delta_1, y_1, sent_1 = scan_piece(1, x_later)
    gate_other = [
        lax.ppermute(run_pick(core_arr, gate_input, piece, width), "core", swap)
        for piece in range(PIECES)
    ]
    enter_0, sent_1 = lax.optimization_barrier((enter_0, sent_1))
    enter_1 = exchange(sent_1, 1)
    full, theirs_0 = run_correct(
        core_arr, None, delta_0, y_0, enter_0, params, read, gate_input, gate_other[0], 0, width
    )
    back_0 = lax.ppermute(theirs_0, "core", swap)
    full, theirs_1 = run_correct(
        core_arr, full, delta_1, y_1, enter_1, params, read, gate_input, gate_other[1], 1, width
    )
    back_1 = lax.ppermute(theirs_1, "core", swap)
    full = run_place(core_arr, full, back_0, 0, width)
    mamba_output = run_place(core_arr, full, back_1, 1, width)
    return (mamba_output, attention_output)


def gather_blocks(rows, blk, blk_count):
    count = rows.shape[0]
    total = jnp.zeros((blk_count * count, rows.shape[1]), rows.dtype)
    total = lax.dynamic_update_slice_in_dim(total, rows, blk * count, 0)
    for flip in range(1, blk_count):
        pairs = [(i, i ^ flip) for i in range(blk_count)]
        got = lax.ppermute(rows, "blk", pairs)
        total = lax.dynamic_update_slice_in_dim(total, got, (blk ^ flip) * count, 0)
    return total


def solution(mesh):
    blk_count = mesh.shape["blk"]
    ulys_count = mesh.shape["ulys"]
    fine = Mesh(
        mesh.devices.reshape(blk_count, ulys_count // PAIR, PAIR), ("blk", "chip", "core")
    )
    rows = P(("blk", "chip", "core"), None)
    col = ("chip", "core")
    placed = (
        rows, rows, rows, rows,
        P(None, col), P(col), P(None, col), P(col), P(None, col), P(col),
        rows, rows, rows,
        P(),
    )
    return jax.shard_map(
        local, mesh=fine, in_specs=placed, out_specs=(rows, rows), check_vma=False
    )
```

time: 659 us -> 518 us (0.79)
  local copies, waits for them, and re-layouts: 164 us -> 42.8 us
  blocking collectives: 38.5 us -> 14.7 us
  other arithmetic: 20 us -> 5.52 us
  starting transfers between devices: 29.3 us -> 42.2 us
  waiting for transfers between devices: 88.7 us -> 96.2 us
    dynamic_slice x4 -> x2, local copies, waits for them, and re-layouts: 57.7 us -> 1.22 us  [exchange(): my_rates = lax.dynamic_slice_in_dim(piece_rates, me * share, share, 1)]
    all_to_all x1, waiting for transfers between devices: 49 us -> 0.01 us  [local(): lax.all_to_all(attended, ulys, split_axis=0, concat_axis=1, tiled=True)]
    reshape x6 -> x8, local copies, waits for them, and re-layouts: 45.2 us -> 5.15 us  [the longest x2 3.56 us: exchange(): sent.reshape(2 * STATE, chunks, share).transpose(1, 0, 2)]
    all_gather x3 -> x0, blocking collectives: 38.5 us -> none  [the longest x1 34.2 us: local(): params = lax.all_gather(packed, 'chip', axis=0, tiled=False)]
    all_to_all x3 -> x5, waiting for transfers between devices: 15.3 us -> 49.5 us  [the longest x1 26.5 us: local(): lax.all_to_all(jnp.broadcast_to(tail[None], (chunks, CONV - 1, PIECES * c...]
    all_to_all x1, waiting for transfers between devices: 24.3 us -> 45.3 us  [local(): lax.all_to_all(kv_rows, ulys, split_axis=1, concat_axis=0, tiled=True)]
    unnamed x37 -> x44, local copies, waits for them, and re-layouts: 19.8 us -> 4.03 us
    select_n x2 -> x0, local copies, waits for them, and re-layouts: 15.6 us -> none  [the longest x1 7.83 us: local(): even = jnp.where(core == 0, mine, back)]
  transfers between devices with their start and end apart: 11 -> 21, of which waited for: 4 -> 5; matrix products, arithmetic and copies ran while one was open for 19% -> 8% of each run, Pallas kernels for 45% -> 58%
where the time goes in v2:
time: 518 us; the launch traced here: 517 us
  Pallas kernels  299 us (58%)
  waiting for transfers between devices  96.2 us (19%)
  local copies, waits for them, and re-layouts  42.8 us (8%)
  starting transfers between devices  42.2 us (8%)
  between operations  15.7 us (3%)
  blocking collectives  14.7 us (3%)
  other arithmetic  5.52 us (1%)
    pallas_call x2, Pallas kernels, run_scan(): pl.pallas_call(scan_kernel, grid_spec=pltpu.PrefetchScalarGridSpec(num_sc...  127 us
    pallas_call x2, Pallas kernels, run_correct(): pl.pallas_call(functools.partial(correct_kernel, resumed=resumed), grid_s...  82.8 us
    pallas_call x1, Pallas kernels, run_flash(): pl.pallas_call(functools.partial(flash_kernel, heads=heads, rows=rows), g...  61 us
    all_to_all x1, waiting for transfers between devices, local(): lax.all_to_all(kv_rows, ulys, split_axis=1, concat_axis=0, tiled=True)  45.3 us
    all_to_all x1, waiting for transfers between devices, local(): lax.all_to_all(jnp.broadcast_to(tail[None], (chunks, CONV - 1, PIECES * c...  26.5 us
    all_to_all x1, waiting for transfers between devices, local(): lax.all_to_all(jnp.broadcast_to(packed[None], (chip_count, PARAM_ROWS, sh...  17.5 us
    pallas_call x4, Pallas kernels, run_pick(): pl.pallas_call(copy_kernel, grid_spec=pltpu.PrefetchScalarGridSpec(num_sc...  15.2 us
    all_to_all x1, blocking collectives, exchange(): lax.all_to_all(enter, chips, split_axis=0, concat_axis=0, tiled=True)  14.7 us
  transfers between devices with their start and end apart: 21, of which 5 were waited for; matrix products, arithmetic and copies ran while one was open for 8% of the time, Pallas kernels for 58%

profile of v2, /device:TPU:0, one launch (start us, length us, event | category | flops | bytes accessed | tf_op | source)
XLA Modules:
  0.0 516.7 jit_solution(15288545848178471217)
XLA Ops:
  7.2 1.9 fusion.12
  9.1 3.8 pick_channels.4
  13.5 3.8 pick_channels.5
  17.6 1.0 broadcast_in_dim.138
  18.6 6.2 %all-to-all-start.1 = ((f32[4,24,2048]{2,1,0:T(8,128)}), f32[4,24,2048]{2,1,0:T(8,128)S(1)}, u32[]{:S(2)}, u32[]{:S(2)}) async-start(f32[4,24,2048]{2,1,0:T(8,128)} %broadcast_in_dim.138), calls=%async_computation.1 | async-start | bytes 1572864 | tf_op jit(solution)/shard_map/all_to_all | solution.py:497
  24.8 0.7 all-gather.7.cloned.1.call-update
  25.5 1.0 slice.43
  27.1 1.1 copy.68
  28.2 1.5 all_to_all.68
  29.7 0.9 slice.57
  30.6 0.9 slice.58
  31.5 17.5 %all-to-all-done.1.param_ref.refs_3_.refs_4_ = f32[4,24,2048]{2,1,0:T(8,128)S(1)} async-done(((f32[4,24,2048]{2,1,0:T(8,128)}), f32[4,24,2048]{2,1,0:T(8,128)S(1)}, u32[]{:S(2)}, u32[]{:S(2)}) %all-to-all-start.1) | async-done | bytes 786464 | tf_op jit(solution)/shard_map/all_to_all | solution.py:497
  49.1 3.6 all-to-all-start.5
  52.8 45.3 %all-to-all-done.5 = bf16[256,8,256]{2,0,1:T(8,128)(2,1)S(1)} async-done(((bf16[256,8,256]{2,0,1:T(8,128)(2,1)}), bf16[256,8,256]{2,0,1:T(8,128)(2,1)S(1)}, u32[]{:S(2)}, u32[]{:S(2)}) %all-to-all-start.5) | async-done | bytes 1048608 | tf_op jit(solution)/shard_map/all_to_all | solution.py:562
  98.1 1.4 broadcast_in_dim.133
  99.5 3.7 all-to-all-start
  103.2 3.2 copy.97
  106.4 26.5 %all-to-all-done = bf16[16,3,8192]{2,1,0:T(4,128)(2,1)S(1)} async-done(((bf16[16,3,8192]{2,1,0:T(4,128)(2,1)}), bf16[16,3,8192]{2,1,0:T(4,128)(2,1)S(1)}, u32[]{:S(2)}, u32[]{:S(2)}) %all-to-all-start) | async-done | bytes 786464 | tf_op jit(solution)/shard_map/all_to_all | solution.py:543
  132.9 1.0 copy-done.4
  133.8 3.6 all-to-all-start.2
  138.1 0.7 fusion.14
  139.4 1.7 compare_convert_fusion
  141.3 0.6 fusion.9
  141.9 0.7 select_reduce_fusion.order_ref
  144.4 0.8 broadcast_select_fusion
  145.2 1.8 copy.63.read_ref.refs_4_.refs_5_
  146.9 0.8 copy.62
  147.8 1.1 reshape.149
  149.1 1.3 collective-permute-start.5
  151.1 2.2 collective-permute-start.6
  153.3 2.2 broadcast_in_dim.153
  155.5 1.0 constant_dynamic-update-slice_fusion.2
  156.5 0.9 fusion
  158.3 0.6 copy.87
  158.9 2.6 broadcast_in_dim.141.inject_ref
  161.5 63.6 %token_scan.2 = (f32[32,512,128]{2,1,0:T(8,128)}, bf16[512,4096]{1,0:T(8,128)(2,1)}, bf16[32,4096]{1,0:T(8,128)(2,1)}) custom-call(s32[1]{0:T(128)} %bitcast.core_ref, bf16[256,16384]{1,0:T(8,128)(2,1)} %own_ref.3, bf16[256,4096]{1,0:T(8,128)(2,1)} %collective-permute-done.other_ref, bf16[8,4096]{1,0:T(8,128)(2,1)} %bitcast.98, ...), custom_call_target="tpu_custom_call" | custom-call | tf_op jit(solution)/shard_map/token_scan/pallas_call | solution.py:306
  225.1 1.9 copy.99
  227.0 5.2 %all-to-all-start.3 = ((bf16[16,32,256]{2,1,0:T(8,128)(2,1)}), bf16[16,32,256]{2,1,0:T(8,128)(2,1)S(1)}, u32[]{:S(2)}, u32[]{:S(2)}) async-start(bf16[16,32,256]{2,1,0:T(8,128)(2,1)} %bitcast.73), calls=%async_computation.3 | async-start | bytes 524288 | tf_op jit(solution)/shard_map/all_to_all | solution.py:575
  232.3 2.3 constant_dynamic-update-slice_fusion.1
  234.6 2.3 constant_dynamic-update-slice_fusion
  236.8 5.4 %all-to-all-done.3.got_ref = bf16[16,32,256]{2,1,0:T(8,128)(2,1)S(1)} async-done(((bf16[16,32,256]{2,1,0:T(8,128)(2,1)}), bf16[16,32,256]{2,1,0:T(8,128)(2,1)S(1)}, u32[]{:S(2)}, u32[]{:S(2)}) %all-to-all-start.3) | async-done | bytes 262176 | tf_op jit(solution)/shard_map/all_to_all | solution.py:575
  242.3 0.7 copy-done.9
  243.0 2.5 state_combine.2
  245.5 3.5 all-to-all-start.4
  249.1 2.3 constant_dynamic-update-slice_fusion.3.kv_ref
  251.3 0.7 copy.90
  252.0 61.0 %causal_attention.1 = bf16[2048,512]{1,0:T(8,128)(2,1)} custom-call(s32[9]{0:T(128)} %compare_convert_fusion.2.side_ref, s32[9]{0:T(128)} %select_reduce_fusion.1.block_ref, s32[9]{0:T(128)} %get-tuple-element.47.diag_ref.last_ref, s32[9]{0:T(128)} %get-tuple-element.46.first_ref, s32[9]{0:T(128)} %get-tuple-element.47.diag_ref.last_ref, ...), custom_call_target="tpu_custom_call" | custom-call | tf_op jit(solution)/shard_map/causal_attention/pallas_call | solution.py:420
  313.0 63.4 %token_scan.3 = (f32[32,512,128]{2,1,0:T(8,128)}, bf16[512,4096]{1,0:T(8,128)(2,1)}, bf16[32,4096]{1,0:T(8,128)(2,1)}) custom-call(s32[1]{0:T(128)} %bitcast.core_ref, bf16[256,16384]{1,0:T(8,128)(2,1)} %own_ref.3, bf16[256,4096]{1,0:T(8,128)(2,1)} %collective-permute-done.1.other_ref, bf16[8,4096]{1,0:T(8,128)(2,1)} %bitcast.97, ...), custom_call_target="tpu_custom_call" | custom-call | tf_op jit(solution)/shard_map/token_scan/pallas_call | solution.py:306
  376.4 0.7 copy.83
  377.1 1.7 copy.98
  378.7 6.9 %all-to-all-start.6 = ((bf16[16,32,256]{2,1,0:T(8,128)(2,1)}), bf16[16,32,256]{2,1,0:T(8,128)(2,1)S(1)}, u32[]{:S(2)}, u32[]{:S(2)}) async-start(bf16[16,32,256]{2,1,0:T(8,128)(2,1)} %bitcast.71), calls=%async_computation.6 | async-start | bytes 524288 | tf_op jit(solution)/shard_map/all_to_all | solution.py:575
  385.6 3.8 pick_channels.6
  389.4 3.9 pick_channels.7
  394.4 0.7 copy-done.8
  395.1 2.5 state_combine.3
  397.7 14.7 %all_to_all.87 = bf16[16,16,256]{2,1,0:T(8,128)(2,1)S(1)} all-to-all(bf16[16,16,256]{2,1,0:T(8,128)(2,1)} %state_combine.3), channel_id=1, replica_groups=mesh['blk'=4,'chip'=4,'core'=2] {'blk','chip'}, dimensions={0} | all-to-all | bytes 262144 | tf_op jit(solution)/shard_map/all_to_all | solution.py:583
  412.4 3.6 all-to-all-start.8
  416.0 41.7 %state_correction.2 = (bf16[256,16384]{1,0:T(8,128)(2,1)}, bf16[256,4096]{1,0:T(8,128)(2,1)}) custom-call(s32[1]{0:T(128)} %bitcast.core_ref, f32[32,512,128]{2,1,0:T(8,128)} %get-tuple-element.18.refs_0_, bf16[512,4096]{1,0:T(8,128)(2,1)} %get-tuple-element.19.refs_1_, bf16[16,4096]{1,0:T(8,128)(2,1)} %bitcast.89, f32[4,24,2048]{2,1,0:T(8,128)} %copy-done, ...), custom_call_target="tpu_custom_call" | custom-call | tf_op jit(solution)/shard_map/state_correction/pallas_call | solution.py:355
  458.2 0.7 copy.85
  458.9 41.1 %state_correction.3 = (bf16[256,16384]{1,0:T(8,128)(2,1)}, bf16[256,4096]{1,0:T(8,128)(2,1)}) custom-call(s32[1]{0:T(128)} %bitcast.core_ref, bf16[256,16384]{1,0:T(8,128)(2,1)} %get-tuple-element.26.refs_0_, f32[32,512,128]{2,1,0:T(8,128)} %get-tuple-element.27.refs_1_, ...), custom_call_target="tpu_custom_call", output_to_operand_aliasing={{0}: (1, {})} | custom-call | tf_op jit(solution)/shard_map/state_correction/pallas_call | solution.py:355
  500.1 3.8 place_channels.2.buffer_ref
  503.8 0.7 collective-permute-done.10.in_ref
  504.5 3.8 place_channels.3
  508.3 1.6 copy.86
  (97 shorter events, 7.1 us)
Async XLA Ops:
  7.2 151.7 %all-gather.5.cloned.1.call-start = ((), (), s32[]{:S(2)}) async-start(), calls=%async_computation.9 | async-start | bytes 4456448 | tf_op jit(solution)/shard_map/all_gather | solution.py:482
  12.9 4.6 copy-start.12
  12.9 4.6 copy-start.13
  12.9 4.6 copy-start.15
  12.9 4.6 copy-start.16
  12.9 4.6 copy-start.17
  13.0 13.7 %copy-start.10 = (bf16[256,1024]{1,0:T(8,128)(2,1)S(1)}, bf16[256,1024]{1,0:T(8,128)(2,1)}, u32[]{:S(2)}) copy-start(bf16[256,1024]{1,0:T(8,128)(2,1)} %param.25) | copy-start | bytes 1572868
  13.0 16.7 %collective-permute-start = (bf16[256,4096]{1,0:T(8,128)(2,1)}, bf16[256,4096]{1,0:T(8,128)(2,1)}, u32[]{:S(2)}, u32[]{:S(2)}) collective-permute-start(bf16[256,4096]{1,0:T(8,128)(2,1)} %pick_channels.4), channel_id=1, source_target_pairs={{0,1},{1,0},{2,3},{3,2},{4,5},{5,4},{6,7},{7,6},{8,9},{9,8},{10,11... | collective-permute-start | bytes 6291464 | tf_op jit(solution)/shard_map/ppermute | solution.py:504
  17.3 9.5 %copy-start.11 = (bf16[256,1024]{1,0:T(8,128)(2,1)S(1)}, bf16[256,1024]{1,0:T(8,128)(2,1)}, u32[]{:S(2)}) copy-start(bf16[256,1024]{1,0:T(8,128)(2,1)} %param.26) | copy-start | bytes 1572868
  17.3 13.3 %collective-permute-start.1 = (bf16[256,4096]{1,0:T(8,128)(2,1)}, bf16[256,4096]{1,0:T(8,128)(2,1)}, u32[]{:S(2)}, u32[]{:S(2)}) collective-permute-start(bf16[256,4096]{1,0:T(8,128)(2,1)} %pick_channels.5), channel_id=1, source_target_pairs={{0,1},{1,0},{2,3},{3,2},{4,5},{5,4},{6,7},{7,6},{8,9},{9,8},{10,11... | collective-permute-start | bytes 6291464 | tf_op jit(solution)/shard_map/ppermute | solution.py:504
  18.6 30.5 %all-to-all-start.1 = ((f32[4,24,2048]{2,1,0:T(8,128)}), f32[4,24,2048]{2,1,0:T(8,128)S(1)}, u32[]{:S(2)}, u32[]{:S(2)}) async-start(f32[4,24,2048]{2,1,0:T(8,128)} %broadcast_in_dim.138), calls=%async_computation.1 | async-start | bytes 1572864 | tf_op jit(solution)/shard_map/all_to_all | solution.py:497
  24.8 288.2 %all-gather.7.cloned.1.call-start = ((), (), s32[]{:S(2)}) async-start(), calls=%async_computation.10 | async-start | bytes 4456448 | tf_op jit(solution)/shard_map/all_gather | solution.py:482
  49.1 99.9 %copy-start = (f32[4,24,2048]{2,1,0:T(8,128)}, f32[4,24,2048]{2,1,0:T(8,128)S(1)}, u32[]{:S(2)}) copy-start(f32[4,24,2048]{2,1,0:T(8,128)S(1)} %all-to-all-done.1.param_ref.refs_3_.refs_4_) | copy-start | bytes 2359300
  49.1 49.1 %all-to-all-start.5 = ((bf16[256,8,256]{2,0,1:T(8,128)(2,1)}), bf16[256,8,256]{2,0,1:T(8,128)(2,1)S(1)}, u32[]{:S(2)}, u32[]{:S(2)}) async-start(bf16[256,8,256]{2,0,1:T(8,128)(2,1)} %all_to_all.68), calls=%async_computation.5 | async-start | bytes 2097152 | tf_op jit(solution)/shard_map/all_to_all | solution.py:562
  98.1 34.7 %copy-start.2 = (bf16[256,8,256]{2,0,1:T(8,128)(2,1)}, bf16[256,8,256]{2,0,1:T(8,128)(2,1)S(1)}, u32[]{:S(2)}) copy-start(bf16[256,8,256]{2,0,1:T(8,128)(2,1)S(1)} %all-to-all-done.5) | copy-start | bytes 3145732
  99.5 33.4 %all-to-all-start = ((bf16[16,3,8192]{2,1,0:T(4,128)(2,1)}), bf16[16,3,8192]{2,1,0:T(4,128)(2,1)S(1)}, u32[]{:S(2)}, u32[]{:S(2)}) async-start(bf16[16,3,8192]{2,1,0:T(4,128)(2,1)} %broadcast_in_dim.133), calls=%async_computation | async-start | bytes 2097152 | tf_op jit(solution)/shard_map/all_to_all | solution.py:543
  103.2 34.3 %copy-start.14 = (bf16[256,32]{0,1:T(8,128)(2,1)S(1)}, bf16[256,32]{0,1:T(8,128)(2,1)}, u32[]{:S(2)}) copy-start(bf16[256,32]{0,1:T(8,128)(2,1)} %param.17) | copy-start | bytes 49156
  103.2 34.7 %copy-start.6 = (bf16[256,512]{1,0:T(8,128)(2,1)S(1)}, bf16[256,512]{1,0:T(8,128)(2,1)}, u32[]{:S(2)}) copy-start(bf16[256,512]{1,0:T(8,128)(2,1)} %low_own_ref.3) | copy-start | bytes 786436
  103.2 34.8 %copy-start.18 = (s32[8]{0:T(128)S(1)}, s32[8]{0:T(128)}, u32[]{:S(2)}) copy-start(s32[8]{0:T(128)} %param.27) | copy-start | bytes 100
  132.9 1.0 copy-start.4
  133.8 91.3 %all-to-all-start.2 = ((bf16[256,8,512]{2,0,1:T(8,128)(2,1)}), bf16[256,8,512]{2,0,1:T(8,128)(2,1)S(1)}, u32[]{:S(2)}, u32[]{:S(2)}) async-start(bf16[256,8,512]{2,0,1:T(8,128)(2,1)} %bitcast.76), calls=%async_computation.2 | async-start | bytes 4194304 | tf_op jit(solution)/shard_map/all_to_all | solution.py:564
  137.5 6.9 %collective-permute-start.3 = (bf16[256,32]{0,1:T(8,128)(2,1)S(1)}, bf16[256,32]{0,1:T(8,128)(2,1)S(1)}, u32[]{:S(2)}, u32[]{:S(2)}) collective-permute-start(bf16[256,32]{0,1:T(8,128)(2,1)S(1)} %copy-done.14), channel_id=1, source_target_pairs={{0,1},{1,0},{2,3},{3,2},{4,5},{5,4},{6,7},{7,6},{8,9},{9,8},{10,11... | collective-permute-start | bytes 49160 | tf_op jit(solution)/shard_map/ppermute | solution.py:508
  137.9 21.1 %collective-permute-start.2 = (bf16[256,512]{1,0:T(8,128)(2,1)S(1)}, bf16[256,512]{1,0:T(8,128)(2,1)S(1)}, u32[]{:S(2)}, u32[]{:S(2)}) collective-permute-start(bf16[256,512]{1,0:T(8,128)(2,1)S(1)} %copy-done.6), channel_id=1, source_target_pairs={{0,1},{1,0},{2,3},{3,2},{4,5},{5,4},{6,7},{7,6},{8,9},{9,8},{10,11... | collective-permute-start | bytes 786440 | tf_op jit(solution)/shard_map/ppermute | solution.py:507
  148.9 6.6 %copy-start.3 = (bf16[256,8,256]{2,0,1:T(8,128)(2,1)S(1)}, bf16[256,8,256]{2,0,1:T(8,128)(2,1)}, u32[]{:S(2)}) copy-start(bf16[256,8,256]{2,0,1:T(8,128)(2,1)} %copy-done.2) | copy-start | bytes 3145732
  148.9 83.4 %collective-permute-start.4 = (bf16[2048,256]{1,0:T(8,128)(2,1)}, bf16[2048,256]{1,0:T(8,128)(2,1)}, u32[]{:S(2)}, u32[]{:S(2)}) collective-permute-start(bf16[2048,256]{1,0:T(8,128)(2,1)} %bitcast.78), channel_id=1, source_target_pairs={{0,8},{8,0},{16,24},{24,16},{1,9},{9,1},{17,25},{25,17},{2,10},{10... | collective-permute-start | bytes 3145736 | tf_op jit(solution)/shard_map/ppermute | solution.py:618
  149.1 7.5 %copy-start.5 = (bf16[16,3,8192]{2,1,0:T(4,128)(2,1)S(1)}, bf16[16,3,8192]{2,1,0:T(4,128)(2,1)}, u32[]{:S(2)}) copy-start(bf16[16,3,8192]{2,1,0:T(4,128)(2,1)} %copy-done.4) | copy-start | bytes 2359300
  149.1 85.5 %collective-permute-start.5 = (bf16[2048,256]{1,0:T(8,128)(2,1)}, bf16[2048,256]{1,0:T(8,128)(2,1)}, u32[]{:S(2)}, u32[]{:S(2)}) collective-permute-start(bf16[2048,256]{1,0:T(8,128)(2,1)} %bitcast.79), channel_id=1, source_target_pairs={{0,16},{8,24},{16,0},{24,8},{1,17},{9,25},{17,1},{25,9},{2,18},{10... | collective-permute-start | bytes 3145736 | tf_op jit(solution)/shard_map/ppermute | solution.py:618
  151.1 98.0 %collective-permute-start.6 = (bf16[2048,256]{1,0:T(8,128)(2,1)}, bf16[2048,256]{1,0:T(8,128)(2,1)}, u32[]{:S(2)}, u32[]{:S(2)}) collective-permute-start(bf16[2048,256]{1,0:T(8,128)(2,1)} %bitcast.80), channel_id=1, source_target_pairs={{0,24},{8,16},{16,8},{24,0},{1,25},{9,17},{17,9},{25,1},{2,26},{10... | collective-permute-start | bytes 3145736 | tf_op jit(solution)/shard_map/ppermute | solution.py:618
  158.9 2.6 copy-start.7
  225.1 26.9 %copy-start.1 = (bf16[256,8,512]{2,0,1:T(8,128)(2,1)}, bf16[256,8,512]{2,0,1:T(8,128)(2,1)S(1)}, u32[]{:S(2)}) copy-start(bf16[256,8,512]{2,0,1:T(8,128)(2,1)S(1)} %all-to-all-done.2) | copy-start | bytes 6291460
  227.0 15.2 %all-to-all-start.3 = ((bf16[16,32,256]{2,1,0:T(8,128)(2,1)}), bf16[16,32,256]{2,1,0:T(8,128)(2,1)S(1)}, u32[]{:S(2)}, u32[]{:S(2)}) async-start(bf16[16,32,256]{2,1,0:T(8,128)(2,1)} %bitcast.73), calls=%async_computation.3 | async-start | bytes 524288 | tf_op jit(solution)/shard_map/all_to_all | solution.py:575
  242.3 0.7 copy-start.9
  245.5 130.9 %all-to-all-start.4 = ((bf16[16,16,256]{2,1,0:T(8,128)(2,1)}), bf16[16,16,256]{2,1,0:T(8,128)(2,1)S(1)}, u32[]{:S(2)}, u32[]{:S(2)}) async-start(bf16[16,16,256]{2,1,0:T(8,128)(2,1)} %state_combine.2), calls=%async_computation.4 | async-start | bytes 262144 | tf_op jit(solution)/shard_map/all_to_all | solution.py:583
  378.7 15.7 %all-to-all-start.6 = ((bf16[16,32,256]{2,1,0:T(8,128)(2,1)}), bf16[16,32,256]{2,1,0:T(8,128)(2,1)S(1)}, u32[]{:S(2)}, u32[]{:S(2)}) async-start(bf16[16,32,256]{2,1,0:T(8,128)(2,1)} %bitcast.71), calls=%async_computation.6 | async-start | bytes 524288 | tf_op jit(solution)/shard_map/all_to_all | solution.py:575
  389.4 26.6 %collective-permute-start.7 = (bf16[256,4096]{1,0:T(8,128)(2,1)}, bf16[256,4096]{1,0:T(8,128)(2,1)}, u32[]{:S(2)}, u32[]{:S(2)}) collective-permute-start(bf16[256,4096]{1,0:T(8,128)(2,1)} %pick_channels.6), channel_id=1, source_target_pairs={{0,1},{1,0},{2,3},{3,2},{4,5},{5,4},{6,7},{7,6},{8,9},{9,8},{10,11... | collective-permute-start | bytes 6291464 | tf_op jit(solution)/shard_map/ppermute | solution.py:594
  393.3 65.6 %collective-permute-start.8 = (bf16[256,4096]{1,0:T(8,128)(2,1)}, bf16[256,4096]{1,0:T(8,128)(2,1)}, u32[]{:S(2)}, u32[]{:S(2)}) collective-permute-start(bf16[256,4096]{1,0:T(8,128)(2,1)} %pick_channels.7), channel_id=1, source_target_pairs={{0,1},{1,0},{2,3},{3,2},{4,5},{5,4},{6,7},{7,6},{8,9},{9,8},{10,11... | collective-permute-start | bytes 6291464 | tf_op jit(solution)/shard_map/ppermute | solution.py:594
  394.4 0.7 copy-start.8
  412.4 95.9 %all-to-all-start.8 = ((bf16[8,256,512]{2,1,0:T(8,128)(2,1)}), bf16[8,256,512]{2,1,0:T(8,128)(2,1)S(1)}, u32[]{:S(2)}, u32[]{:S(2)}) async-start(bf16[8,256,512]{2,1,0:T(8,128)(2,1)} %bitcast.22), calls=%async_computation.8 | async-start | bytes 4194304 | tf_op jit(solution)/shard_map/all_to_all | solution.py:590
  457.8 42.3 %collective-permute-start.9 = (bf16[256,4096]{1,0:T(8,128)(2,1)}, bf16[256,4096]{1,0:T(8,128)(2,1)}, u32[]{:S(2)}, u32[]{:S(2)}) collective-permute-start(bf16[256,4096]{1,0:T(8,128)(2,1)} %get-tuple-element.31), channel_id=1, source_target_pairs={{0,1},{1,0},{2,3},{3,2},{4,5},{5,4},{6,7},{7,6},{8,9},{9,8},{10,11... | collective-permute-start | bytes 6291464 | tf_op jit(solution)/shard_map/ppermute | solution.py:602
  500.0 4.5 collective-permute-start.10
Sparse Core Ops, SparseCore 0:
  10.7 107.6 all-gather.4
  121.2 109.8 all-gather.6
